TPU v7x, 32 devices: a whole 2x2x4 slice. The times are simulated.
32 devices in a mesh: scan: 2 (over x), row: 16 (over z, y, core).
Axes of the slice: x: 2, y: 2, z: 4, core: 2. Of those that a mesh axis runs over, the one named last changes fastest.
Arguments:
- object_field: float32 [2, 2, 4096, 768], P(None, None, ('scan', 'row')), parts along dimension 2, may hold values from -1 to 1
- row_offset: int32 [32], P(('scan', 'row')), parts along dimension 0, may hold values from 0 to 127
- col_offset: int32 [32], P(('scan', 'row')), parts along dimension 0, may hold values from 0 to 256
- amplitudes: float32 [32, 512, 512], P(('scan', 'row')), parts along dimension 0, may hold values from 0.2 to 2
- probe: float32 [4, 512, 512], P('scan'), parts along dimension 0, may hold values from -6 to 6
- phase: float32 [512, 512], replicated, may hold values from -3.140625 to 3.140625
Outputs:
- updated_object: float32 [2, 2, 4096, 768], P(None, None, ('scan', 'row')), parts along dimension 2
There are 2 independent parts, one for each index of `scan`. A program takes and returns all parts, laid end to end along the dimension named above; an argument that names none is the same for every part. Nothing has to cross between parts.
All inputs are finite; a program needn't handle non-finite values.
Results may differ from a plain program's by a relative error of at most 0.014.
Values sent between devices are 32-bit elements; how exact they have to be, the bound alone decides.
A program may use at most 64 MiB of HBM per device.

v0:
```python
import math

import jax
import jax.numpy as jnp
from jax import lax
from jax.sharding import PartitionSpec as P


def shifted(block, axis, distance):
    devices = range(lax.axis_size(axis))
    route = [((i - distance) % len(devices), i) for i in devices]
    return lax.ppermute(block, axis, route)


def dft_mats(length, flip):
    index = jnp.arange(length, dtype=jnp.int32)
    angles = (index[:, None] * index[None, :] % length).astype(jnp.float32) * (
        -2.0 * math.pi / length
    )
    factor = 1.0 / math.sqrt(length)
    cos_table = (jnp.cos(angles) * factor).astype(jnp.bfloat16)
    sin_table = (jnp.sin(angles) * factor).astype(jnp.bfloat16)
    if flip:
        sin_table = -sin_table
    left_real = jnp.concatenate([cos_table, -sin_table], axis=1)
    left_imag = jnp.concatenate([sin_table, cos_table], axis=1)
    right_real = jnp.concatenate([cos_table, -sin_table], axis=0)
    right_imag = jnp.concatenate([sin_table, cos_table], axis=0)
    return (left_real, left_imag, right_real, right_imag)


def transform(real_part, imag_part, mats):
    left_real, left_imag, right_real, right_imag = mats
    stacked = jnp.concatenate(
        [real_part.astype(jnp.bfloat16), imag_part.astype(jnp.bfloat16)], axis=0
    )
    half_real = jnp.dot(left_real, stacked, preferred_element_type=jnp.float32).astype(jnp.bfloat16)
    half_imag = jnp.dot(left_imag, stacked, preferred_element_type=jnp.float32).astype(jnp.bfloat16)
    joined = jnp.concatenate([half_real, half_imag], axis=1)
    return (
        jnp.dot(joined, right_real, preferred_element_type=jnp.float32),
        jnp.dot(joined, right_imag, preferred_element_type=jnp.float32),
    )


def cmul(a_real, a_imag, b_real, b_imag):
    return (a_real * b_real - a_imag * b_imag, a_real * b_imag + a_imag * b_real)


def cmul_conj(a_real, a_imag, b_real, b_imag):
    return (a_real * b_real + a_imag * b_imag, a_real * b_imag - a_imag * b_real)


def window_gradient(window, probe, amplitude, phase, forward, inverse):
    prop_real = jnp.cos(phase)
    prop_imag = jnp.sin(phase)
    probe_real, probe_imag = (probe[0], probe[1])
    first_real, first_imag = (window[0, 0], window[0, 1])
    second_real, second_imag = (window[1, 0], window[1, 1])
    exit_real, exit_imag = cmul(probe_real, probe_imag, first_real, first_imag)
    freq_real, freq_imag = transform(exit_real, exit_imag, forward)
    moved_real, moved_imag = cmul(freq_real, freq_imag, prop_real, prop_imag)
    inner_real, inner_imag = transform(moved_real, moved_imag, inverse)
    wave_real, wave_imag = cmul(inner_real, inner_imag, second_real, second_imag)
    far_real, far_imag = transform(wave_real, wave_imag, forward)
    modulus = jnp.sqrt(far_real * far_real + far_imag * far_imag)
    ratio = amplitude / jnp.maximum(modulus, 0.1)
    resid_real = far_real * (1.0 - ratio)
    resid_imag = far_imag * (1.0 - ratio)
    back_real, back_imag = transform(resid_real, resid_imag, inverse)
    grad2_real, grad2_imag = cmul_conj(inner_real, inner_imag, back_real, back_imag)
    mid_real, mid_imag = cmul_conj(second_real, second_imag, back_real, back_imag)
    spec_real, spec_imag = transform(mid_real, mid_imag, forward)
    unprop_real, unprop_imag = cmul_conj(prop_real, prop_imag, spec_real, spec_imag)
    entry_real, entry_imag = transform(unprop_real, unprop_imag, inverse)
    grad1_real, grad1_imag = cmul_conj(probe_real, probe_imag, entry_real, entry_imag)
    return jnp.stack([jnp.stack([grad1_real, grad1_imag]), jnp.stack([grad2_real, grad2_imag])])


def add_into(total, piece, row_lo, col_lo):
    anchor = jnp.int32(0)
    spot = (anchor, anchor, jnp.int32(row_lo), col_lo)
    current = lax.dynamic_slice(total, spot, piece.shape)
    return lax.dynamic_update_slice(total, current + piece, spot)


def body(object_field, row_offset, col_offset, amplitudes, probe, phase):
    strip_rows = object_field.shape[2]
    window_edge = probe.shape[1]
    half_rows = strip_rows // 2
    anchor = jnp.int32(0)
    forward = dft_mats(window_edge, False)
    inverse = dft_mats(window_edge, True)
    all_columns = lax.all_gather(col_offset, "row", axis=0, tiled=True)
    position = lax.axis_index("row")
    count = lax.axis_size("row")

    def column_of(lag):
        return all_columns[(position - lag + count) % count]

    def carve(lag, row_lo, row_count):
        return lax.dynamic_slice(
            object_field,
            (anchor, anchor, jnp.int32(row_lo), column_of(lag)),
            (2, 2, row_count, window_edge),
        )

    own_col = col_offset[0]
    pieces = {
        0: lax.dynamic_slice(
            object_field, (anchor, anchor, anchor, own_col), (2, 2, strip_rows, window_edge)
        )
    }
    for owner in (-1, 1, 2):
        pieces[owner] = shifted(carve(owner, 0, strip_rows), "row", -owner)
    for owner, row_lo in ((-2, half_rows), (3, 0)):
        pieces[owner] = shifted(carve(owner, row_lo, half_rows), "row", -owner)
    trimmed = jnp.concatenate([pieces[owner] for owner in (-2, -1, 0, 1, 2, 3)], axis=2)
    row_start = row_offset[0]
    window = lax.dynamic_slice(
        trimmed, (anchor, anchor, row_start, anchor), (2, 2, window_edge, window_edge)
    )
    grads = window_gradient(window, probe, amplitudes[0], phase, forward, inverse)
    canvas = jnp.zeros(trimmed.shape, jnp.float32)
    canvas = lax.dynamic_update_slice(canvas, grads, (anchor, anchor, row_start, anchor))
    bounds = {-2: (0, half_rows)}
    for owner in (-1, 0, 1, 2):
        lower = half_rows + (owner + 1) * strip_rows
        bounds[owner] = (lower, lower + strip_rows)
    bounds[3] = (half_rows + 4 * strip_rows, 5 * strip_rows)
    blocks = {owner: canvas[:, :, bounds[owner][0] : bounds[owner][1]] for owner in bounds}
    total = jnp.zeros(object_field.shape, jnp.float32)
    total = add_into(total, blocks[0], 0, own_col)
    for owner in (-1, 1, 2):
        arrived = shifted(blocks[owner], "row", owner)
        total = add_into(total, arrived, 0, column_of(owner))
    for owner, row_lo in ((-2, half_rows), (3, 0)):
        arrived = shifted(blocks[owner], "row", owner)
        total = add_into(total, arrived, row_lo, column_of(owner))
    return object_field - 0.5 * total


def solution(mesh):
    placed = (
        P(None, None, ("scan", "row"), None),
        P(("scan", "row")),
        P(("scan", "row")),
        P(("scan", "row"), None, None),
        P("scan", None, None),
        P(),
    )
    return jax.shard_map(
        body,
        mesh=mesh,
        in_specs=placed,
        out_specs=P(None, None, ("scan", "row"), None),
        check_vma=False,
    )
```

profile of v0, /device:TPU:1, one launch (start us, length us, event | category | flops | bytes accessed | tf_op | source)
XLA Modules:
  0.0 250.9 jit_solution(9333258213070651751)
XLA Ops:
  2.8 10.7 %all-reduce = s32[16]{0:T(128)S(1)} all-reduce(s32[16]{0:T(128)S(1)} %dynamic-update-slice), channel_id=1, replica_groups=mesh['scan'=2,'row'=16] {'row'}, use_global_device_ids=true, to_apply=%add | all-reduce | flops 16 | bytes 128
  17.5 3.6 %collective-permute-start.1 = (f32[2,2,128,512]{3,2,1,0:T(8,128)S(1)}, f32[2,2,128,512]{3,2,1,0:T(8,128)}, u32[]{:S(2)}, u32[]{:S(2)}) collective-permute-start(f32[2,2,128,512]{3,2,1,0:T(8,128)S(1)} %constant_dynamic-slice_fusion.3), channel_id=1, source_target_pairs={{15,0},{0,1},{1,2},{2,3},{3,4},{4,5},{5,6},{6,7},{7,8},{8,9},{9,10... | collective-permute-start | bytes 3145736 | tf_op jit(solution)/shard_map/ppermute | solution.py:12
  31.1 16.9 %collective-permute-done = f32[2,2,64,512]{3,2,1,0:T(8,128)S(1)} collective-permute-done((f32[2,2,64,512]{3,2,1,0:T(8,128)}, f32[2,2,64,512]{3,2,1,0:T(8,128)S(1)}, u32[]{:S(2)}, u32[]{:S(2)}) %collective-permute-start) | collective-permute-done | bytes 524320 | tf_op jit(solution)/shard_map/ppermute | solution.py:12
  51.1 2.6 %constant_dynamic-slice_fusion.1 = (f32[2,2,128,512]{3,2,1,0:T(8,128)}, f32[2,2,128,512]{3,2,1,0:T(8,128)}, f32[2,2,640,512]{3,2,1,0:T(8,128)}) fusion(f32[2,2,128,768]{3,2,1,0:T(8,128)S(1)} %copy-done, s32[]{:T(128)S(6)} %select_n.137, s32[]{:T(128)S(6)} %select_n.134, f32[2,2,640,512]{3,2,1,0:T(8,128)} %constant_dynamic-update-slice_fusion.3, ...), kind=kLoop, calls=%fused_computation.106 | loop fusion | bytes 6291468 | tf_op jit(solution)/shard_map/dynamic_slice | solution.py:102
  55.1 4.0 %fusion.27 = bf16[512,512]{1,0:T(8,128)(2,1)S(1)} fusion(), kind=kLoop, calls=%fused_computation.99 | loop fusion | flops 4980736 | bytes 524288 | tf_op jit(solution)/shard_map/neg | solution.py:24
  59.1 4.4 %multiply_convert_fusion.2 = (bf16[512,512]{1,0:T(8,128)(2,1)S(1)}, bf16[512,512]{1,0:T(8,128)(2,1)S(1)}) fusion(), kind=kLoop, calls=%fused_computation.80 | loop fusion | flops 4718592 | bytes 1048576 | tf_op jit(solution)/shard_map/convert_element_type | solution.py:22
  63.5 3.9 %fusion.54 = (f32[512,512]{1,0:T(8,128)S(1)}, f32[512,512]{1,0:T(8,128)S(1)}) fusion(f32[512,512]{1,0:T(8,128)S(1)} %copy-done.2), kind=kLoop, calls=%fused_computation.136 | loop fusion | bytes 3145728 | tf_op jit(solution)/shard_map/sin | solution.py:56
  67.4 12.3 %collective-permute-done.2 = f32[2,2,128,512]{3,2,1,0:T(8,128)} collective-permute-done((f32[2,2,128,512]{3,2,1,0:T(8,128)}, f32[2,2,128,512]{3,2,1,0:T(8,128)}, u32[]{:S(2)}, u32[]{:S(2)}) %collective-permute-start.2) | collective-permute-done | bytes 1048608 | tf_op jit(solution)/shard_map/ppermute | solution.py:12
  84.4 14.6 %collective-permute-done.4 = f32[2,2,64,512]{3,2,1,0:T(8,128)S(1)} collective-permute-done((f32[2,2,64,512]{3,2,1,0:T(8,128)}, f32[2,2,64,512]{3,2,1,0:T(8,128)S(1)}, u32[]{:S(2)}, u32[]{:S(2)}) %collective-permute-start.4) | collective-permute-done | bytes 524320 | tf_op jit(solution)/shard_map/ppermute | solution.py:12
  107.4 2.5 subtract_convert_fusion.2
  128.7 3.0 %broadcast_in_dim.5 = f32[2,2,640,512]{3,2,1,0:T(8,128)} broadcast(f32[]{:T(128)} %constant.80.clone.1), dimensions={} | broadcast | bytes 5242884 | tf_op jit(solution)/shard_map/broadcast_in_dim | solution.py:124
  131.7 13.6 %dynamic_update_slice.21 = f32[2,2,640,512]{3,2,1,0:T(8,128)} dynamic-update-slice(f32[2,2,640,512]{3,2,1,0:T(8,128)} %broadcast_in_dim.5, f32[2,2,512,512]{3,2,1,0:T(8,128)} %pad_maximum_fusion, s32[]{:T(128)} %constant.81.clone.1, s32[]{:T(128)} %constant.81.clone.1, s32[]{:T(128)S(6)} %select_n.141, s32[]{:T(128)} %constant.81.clone.1) | dynamic-update-slice | bytes 8388612 | tf_op jit(solution)/shard_map/dynamic_update_slice | solution.py:125
  145.3 4.3 %fusion.53 = (f32[2,2,128,512]{3,2,1,0:T(8,128)}, f32[2,2,128,512]{3,2,1,0:T(8,128)}, f32[2,2,128,512]{3,2,1,0:T(8,128)}, f32[2,2,128,512]{3,2,1,0:T(8,128)}) fusion(f32[2,2,640,512]{3,2,1,0:T(8,128)} %dynamic_update_slice.21), kind=kLoop, calls=%fused_computation.135 | loop fusion | bytes 8388608 | tf_op jit(solution)/shard_map/slice | solution.py:131
  153.6 4.2 %collective-permute-start.8 = (f32[2,2,64,512]{3,2,1,0:T(8,128)}, f32[2,2,64,512]{3,2,1,0:T(8,128)}, u32[]{:S(2)}, u32[]{:S(2)}) collective-permute-start(f32[2,2,64,512]{3,2,1,0:T(8,128)} %get-tuple-element.12), channel_id=1, source_target_pairs={{2,0},{3,1},{4,2},{5,3},{6,4},{7,5},{8,6},{9,7},{10,8},{11,9},{12,... | collective-permute-start | bytes 1572872 | tf_op jit(solution)/shard_map/ppermute | solution.py:12
  157.9 4.4 %dynamic_update_slice.22 = f32[2,2,128,768]{3,2,1,0:T(8,128)S(1)} dynamic-update-slice(f32[2,2,128,768]{3,2,1,0:T(8,128)S(1)} %broadcast_in_dim.4, f32[2,2,128,512]{3,2,1,0:T(8,128)} %get-tuple-element.16, s32[]{:T(128)} %constant.81.clone.1, s32[]{:T(128)} %constant.81.clone.1, s32[]{:T(128)} %constant.81.clone.1, s32[]{:T(128)S(6)} %select_n.131) | dynamic-update-slice | bytes 2097156 | tf_op jit(solution)/shard_map/dynamic_update_slice | solution.py:84
  162.3 46.7 %collective-permute-done.5 = f32[2,2,128,512]{3,2,1,0:T(8,128)} collective-permute-done((f32[2,2,128,512]{3,2,1,0:T(8,128)}, f32[2,2,128,512]{3,2,1,0:T(8,128)}, u32[]{:S(2)}, u32[]{:S(2)}) %collective-permute-start.5) | collective-permute-done | bytes 1048608 | tf_op jit(solution)/shard_map/ppermute | solution.py:12
  209.1 2.6 %dynamic-slice_add_fusion.2 = f32[2,2,128,512]{3,2,1,0:T(8,128)} fusion(f32[2,2,128,512]{3,2,1,0:T(8,128)} %collective-permute-done.5, f32[2,2,128,768]{3,2,1,0:T(8,128)S(1)} %dynamic_update_slice.22, s32[]{:T(128)S(6)} %select_n.130), kind=kLoop, calls=%fused_computation.66 | loop fusion | flops 262144 | bytes 3145732 | tf_op jit(solution)/shard_map/add | solution.py:84
  211.7 6.2 %dynamic_update_slice.23 = f32[2,2,128,768]{3,2,1,0:T(8,128)S(1)} dynamic-update-slice(f32[2,2,128,768]{3,2,1,0:T(8,128)S(1)} %dynamic_update_slice.22, f32[2,2,128,512]{3,2,1,0:T(8,128)} %dynamic-slice_add_fusion.2, s32[]{:T(128)} %constant.81.clone.1, s32[]{:T(128)} %constant.81.clone.1, s32[]{:T(128)} %constant.81.clone.1, s32[]{:T(128)S(6)} %select_n.130) | dynamic-update-slice | bytes 2097156 | tf_op jit(solution)/shard_map/dynamic_update_slice | solution.py:84
  217.9 2.5 %dynamic-slice_add_fusion.1 = f32[2,2,128,512]{3,2,1,0:T(8,128)} fusion(f32[2,2,128,512]{3,2,1,0:T(8,128)} %collective-permute-done.6, f32[2,2,128,768]{3,2,1,0:T(8,128)S(1)} %dynamic_update_slice.23, s32[]{:T(128)S(6)} %select_n.134), kind=kLoop, calls=%fused_computation.65 | loop fusion | flops 262144 | bytes 3145732 | tf_op jit(solution)/shard_map/add | solution.py:84
  220.5 5.5 %dynamic_update_slice.24 = f32[2,2,128,768]{3,2,1,0:T(8,128)S(1)} dynamic-update-slice(f32[2,2,128,768]{3,2,1,0:T(8,128)S(1)} %dynamic_update_slice.23, f32[2,2,128,512]{3,2,1,0:T(8,128)} %dynamic-slice_add_fusion.1, s32[]{:T(128)} %constant.81.clone.1, s32[]{:T(128)} %constant.81.clone.1, s32[]{:T(128)} %constant.81.clone.1, s32[]{:T(128)S(6)} %select_n.134) | dynamic-update-slice | bytes 2097156 | tf_op jit(solution)/shard_map/dynamic_update_slice | solution.py:84
  226.0 2.5 %dynamic-slice_add_fusion = f32[2,2,128,512]{3,2,1,0:T(8,128)} fusion(f32[2,2,128,512]{3,2,1,0:T(8,128)} %collective-permute-done.7, f32[2,2,128,768]{3,2,1,0:T(8,128)S(1)} %dynamic_update_slice.24, s32[]{:T(128)S(6)} %select_n.137), kind=kLoop, calls=%fused_computation.64 | loop fusion | flops 262144 | bytes 3145732 | tf_op jit(solution)/shard_map/add | solution.py:84
  228.5 5.6 %dynamic_update_slice.25 = f32[2,2,128,768]{3,2,1,0:T(8,128)S(1)} dynamic-update-slice(f32[2,2,128,768]{3,2,1,0:T(8,128)S(1)} %dynamic_update_slice.24, f32[2,2,128,512]{3,2,1,0:T(8,128)} %dynamic-slice_add_fusion, s32[]{:T(128)} %constant.81.clone.1, s32[]{:T(128)} %constant.81.clone.1, s32[]{:T(128)} %constant.81.clone.1, s32[]{:T(128)S(6)} %select_n.137) | dynamic-update-slice | bytes 2097156 | tf_op jit(solution)/shard_map/dynamic_update_slice | solution.py:84
  236.2 5.3 %dynamic_update_slice.26 = f32[2,2,128,768]{3,2,1,0:T(8,128)S(1)} dynamic-update-slice(f32[2,2,128,768]{3,2,1,0:T(8,128)S(1)} %dynamic_update_slice.25, f32[2,2,64,512]{3,2,1,0:T(8,128)} %dynamic-slice_add_fusion.4, s32[]{:T(128)} %constant.81.clone.1, s32[]{:T(128)} %constant.81.clone.1, s32[]{:T(128)} %constant.86.clone.1, s32[]{:T(128)S(6)} %select_n.127) | dynamic-update-slice | bytes 1048580 | tf_op jit(solution)/shard_map/dynamic_update_slice | solution.py:84
  243.6 6.0 %dynamic_update_slice.27 = f32[2,2,128,768]{3,2,1,0:T(8,128)S(1)} dynamic-update-slice(f32[2,2,128,768]{3,2,1,0:T(8,128)S(1)} %dynamic_update_slice.26, f32[2,2,64,512]{3,2,1,0:T(8,128)} %dynamic-slice_add_fusion.3, s32[]{:T(128)} %constant.81.clone.1, s32[]{:T(128)} %constant.81.clone.1, s32[]{:T(128)} %constant.81.clone.1, s32[]{:T(128)S(6)} %select_n.140) | dynamic-update-slice | bytes 1048580 | tf_op jit(solution)/shard_map/dynamic_update_slice | solution.py:84
  (66 shorter events, 51.6 us)
Async XLA Ops:
  0.0 25.1 %copy-start = (f32[2,2,128,768]{3,2,1,0:T(8,128)S(1)}, f32[2,2,128,768]{3,2,1,0:T(8,128)}, u32[]{:S(2)}) copy-start(f32[2,2,128,768]{3,2,1,0:T(8,128)} %param.6) | copy-start | bytes 4718596
  17.5 31.4 %collective-permute-start.1 = (f32[2,2,128,512]{3,2,1,0:T(8,128)S(1)}, f32[2,2,128,512]{3,2,1,0:T(8,128)}, u32[]{:S(2)}, u32[]{:S(2)}) collective-permute-start(f32[2,2,128,512]{3,2,1,0:T(8,128)S(1)} %constant_dynamic-slice_fusion.3), channel_id=1, source_target_pairs={{15,0},{0,1},{1,2},{2,3},{3,4},{4,5},{5,6},{6,7},{7,8},{8,9},{9,10... | collective-permute-start | bytes 3145736 | tf_op jit(solution)/shard_map/ppermute | solution.py:12
  26.5 21.5 %collective-permute-start = (f32[2,2,64,512]{3,2,1,0:T(8,128)}, f32[2,2,64,512]{3,2,1,0:T(8,128)S(1)}, u32[]{:S(2)}, u32[]{:S(2)}) collective-permute-start(f32[2,2,64,512]{3,2,1,0:T(8,128)} %get-tuple-element.30), channel_id=1, source_target_pairs={{14,0},{15,1},{0,2},{1,3},{2,4},{3,5},{4,6},{5,7},{6,8},{7,9},{8,1... | collective-permute-start | bytes 1572872 | tf_op jit(solution)/shard_map/ppermute | solution.py:12
  53.7 9.8 %copy-start.2 = (f32[512,512]{1,0:T(8,128)S(1)}, f32[512,512]{1,0:T(8,128)}, u32[]{:S(2)}) copy-start(f32[512,512]{1,0:T(8,128)} %param.11) | copy-start | bytes 3145732
  53.7 26.0 %collective-permute-start.2 = (f32[2,2,128,512]{3,2,1,0:T(8,128)}, f32[2,2,128,512]{3,2,1,0:T(8,128)}, u32[]{:S(2)}, u32[]{:S(2)}) collective-permute-start(f32[2,2,128,512]{3,2,1,0:T(8,128)} %get-tuple-element.32), channel_id=1, source_target_pairs={{1,0},{2,1},{3,2},{4,3},{5,4},{6,5},{7,6},{8,7},{9,8},{10,9},{11,1... | collective-permute-start | bytes 3145736 | tf_op jit(solution)/shard_map/ppermute | solution.py:12
  53.7 28.3 %collective-permute-start.3 = (f32[2,2,128,512]{3,2,1,0:T(8,128)}, f32[2,2,128,512]{3,2,1,0:T(8,128)}, u32[]{:S(2)}, u32[]{:S(2)}) collective-permute-start(f32[2,2,128,512]{3,2,1,0:T(8,128)} %get-tuple-element.31), channel_id=1, source_target_pairs={{2,0},{3,1},{4,2},{5,3},{6,4},{7,5},{8,6},{9,7},{10,8},{11,9},{12,... | collective-permute-start | bytes 3145736 | tf_op jit(solution)/shard_map/ppermute | solution.py:12
  53.7 45.3 %collective-permute-start.4 = (f32[2,2,64,512]{3,2,1,0:T(8,128)}, f32[2,2,64,512]{3,2,1,0:T(8,128)S(1)}, u32[]{:S(2)}, u32[]{:S(2)}) collective-permute-start(f32[2,2,64,512]{3,2,1,0:T(8,128)} %get-tuple-element.29), channel_id=1, source_target_pairs={{3,0},{4,1},{5,2},{6,3},{7,4},{8,5},{9,6},{10,7},{11,8},{12,9},{13... | collective-permute-start | bytes 1572872 | tf_op jit(solution)/shard_map/ppermute | solution.py:12
  82.0 17.9 %copy-start.1 = (f32[2,512,512]{2,1,0:T(8,128)S(1)}, f32[2,512,512]{2,1,0:T(8,128)}, u32[]{:S(2)}) copy-start(f32[2,512,512]{2,1,0:T(8,128)} %param.10) | copy-start | bytes 6291460
  111.5 1.2 copy-start.3
  149.6 59.5 %collective-permute-start.5 = (f32[2,2,128,512]{3,2,1,0:T(8,128)}, f32[2,2,128,512]{3,2,1,0:T(8,128)}, u32[]{:S(2)}, u32[]{:S(2)}) collective-permute-start(f32[2,2,128,512]{3,2,1,0:T(8,128)} %get-tuple-element.15), channel_id=1, source_target_pairs={{1,0},{2,1},{3,2},{4,3},{5,4},{6,5},{7,6},{8,7},{9,8},{10,9},{11,1... | collective-permute-start | bytes 3145736 | tf_op jit(solution)/shard_map/ppermute | solution.py:12
  150.4 67.5 %collective-permute-start.6 = (f32[2,2,128,512]{3,2,1,0:T(8,128)}, f32[2,2,128,512]{3,2,1,0:T(8,128)}, u32[]{:S(2)}, u32[]{:S(2)}) collective-permute-start(f32[2,2,128,512]{3,2,1,0:T(8,128)} %get-tuple-element.14), channel_id=1, source_target_pairs={{15,0},{0,1},{1,2},{2,3},{3,4},{4,5},{5,6},{6,7},{7,8},{8,9},{9,10... | collective-permute-start | bytes 3145736 | tf_op jit(solution)/shard_map/ppermute | solution.py:12
  151.3 74.7 %collective-permute-start.7 = (f32[2,2,128,512]{3,2,1,0:T(8,128)}, f32[2,2,128,512]{3,2,1,0:T(8,128)}, u32[]{:S(2)}, u32[]{:S(2)}) collective-permute-start(f32[2,2,128,512]{3,2,1,0:T(8,128)} %get-tuple-element.13), channel_id=1, source_target_pairs={{14,0},{15,1},{0,2},{1,3},{2,4},{3,5},{4,6},{5,7},{6,8},{7,9},{8,1... | collective-permute-start | bytes 3145736 | tf_op jit(solution)/shard_map/ppermute | solution.py:12
  153.6 80.5 %collective-permute-start.8 = (f32[2,2,64,512]{3,2,1,0:T(8,128)}, f32[2,2,64,512]{3,2,1,0:T(8,128)}, u32[]{:S(2)}, u32[]{:S(2)}) collective-permute-start(f32[2,2,64,512]{3,2,1,0:T(8,128)} %get-tuple-element.12), channel_id=1, source_target_pairs={{2,0},{3,1},{4,2},{5,3},{6,4},{7,5},{8,6},{9,7},{10,8},{11,9},{12,... | collective-permute-start | bytes 1572872 | tf_op jit(solution)/shard_map/ppermute | solution.py:12
  157.8 83.8 %collective-permute-start.9 = (f32[2,2,64,512]{3,2,1,0:T(8,128)}, f32[2,2,64,512]{3,2,1,0:T(8,128)}, u32[]{:S(2)}, u32[]{:S(2)}) collective-permute-start(f32[2,2,64,512]{3,2,1,0:T(8,128)} %get-tuple-element.11), channel_id=1, source_target_pairs={{13,0},{14,1},{15,2},{0,3},{1,4},{2,5},{3,6},{4,7},{5,8},{6,9},{7,... | collective-permute-start | bytes 1572872 | tf_op jit(solution)/shard_map/ppermute | solution.py:12
where the time goes:
time: 253 us; the launch traced here: 251 us
  waiting for transfers between devices  90.6 us (36%)
  local copies, waits for them, and re-layouts  77.7 us (31%)
  other arithmetic  28.9 us (11%)
  matrix products  20.7 us (8%)
  between operations  11.3 us (4%)
  starting transfers between devices  11 us (4%)
  blocking collectives  10.7 us (4%)
    ppermute x10, waiting for transfers between devices, shifted(): return lax.ppermute(block, axis, route)  90.6 us
    dynamic_update_slice x6, local copies, waits for them, and re-layouts, add_into(): return lax.dynamic_update_slice(total, current + piece, spot)  33 us
    dynamic_update_slice x1, local copies, waits for them, and re-layouts, body(): lax.dynamic_update_slice(canvas, grads, (anchor, anchor, row_start, anchor))  13.6 us
    add x5, other arithmetic, add_into(): return lax.dynamic_update_slice(total, current + piece, spot)  11.8 us
    ppermute x10, starting transfers between devices, shifted(): return lax.ppermute(block, axis, route)  11 us
    unnamed x1, blocking collectives  10.7 us
    unnamed x15, local copies, waits for them, and re-layouts  10.3 us
    slice x2, local copies, waits for them, and re-layouts, body(): canvas[:, :, bounds[owner][0]:bounds[owner][1]]  6.53 us
  transfers between devices with their start and end apart: 10, of which 4 were waited for; matrix products, arithmetic and copies ran while one was open for 23% of the time, Pallas kernels for 0%

commit v1 on v0

v1 whole, which is shorter than its diff:
```python
import functools
import math

import jax
import jax.numpy as jnp
from jax import lax
from jax.experimental import pallas as pl
from jax.experimental.pallas import tpu as pltpu
from jax.sharding import PartitionSpec as P

MESH = pl.DeviceIdType.MESH

M2, M1, OWN, P1, P2, P3 = range(6)
EDGES = {
    0: (
        (OWN, 0, "y", M2), (OWN, 1, -3, P3), (OWN, 0, "c", M1),
        (P2, 2, 4, M2), (P2, 0, "c", P1), (M1, 2, "c", M2),
    ),
    1: (
        (OWN, 0, "y", M2), (OWN, 0, "c", P1),
        (P2, 0, 3, M1), (P2, 1, "c", P3),
    ),
    2: (
        (OWN, 0, "y", P2), (OWN, 1, -3, P3), (OWN, 0, "c", M1),
        (M2, 0, -4, P2), (P2, 0, "c", P1),
    ),
    3: (
        (OWN, 0, "y", P2), (OWN, 0, "c", P1),
        (M2, 0, -4, P2), (M2, 0, "c", M1), (P2, 1, "c", P3),
    ),
}
BACK = {"y": "y", "c": "c", 3: -3, -3: 3, 4: -4, -4: 4}
MAX_EDGES = max(len(edges) for edges in EDGES.values())


def role_at(role, target):
    if target == "y":
        return role ^ 2
    if target in ("c", 3, -3):
        return role ^ 1
    return role


def arrivals():
    table = {role: {} for role in EDGES}
    for role, edges in EDGES.items():
        for number, (source, half, target, slot) in enumerate(edges):
            table[role_at(role, target)][slot] = (BACK[target], number, half)
    return table


ARRIVE = arrivals()


def place(target):
    me, count = lax.axis_index("row"), lax.axis_size("row")
    if target == "y":
        return me + 2 - 4 * (me // 2 % 2)
    if target == "c":
        return me + 1 - 2 * (me % 2)
    return (me + target + count) % count


def rows_of(slot, half, strip):
    if half == 0:
        return pl.ds(slot * strip, strip)
    return pl.ds(slot * strip + (half - 1) * (strip // 2), strip // 2)


def greet():
    me = lax.axis_index("row")
    barrier = pltpu.get_barrier_semaphore()
    for target in ("y", "c", 4, -4):
        pl.semaphore_signal(barrier, inc=1, device_id={"row": place(target)}, device_id_type=MESH)

    @pl.when(me % 2 == 0)
    def _():
        pl.semaphore_signal(barrier, inc=1, device_id={"row": place(-3)}, device_id_type=MESH)

    @pl.when(me % 2 == 1)
    def _():
        pl.semaphore_signal(barrier, inc=1, device_id={"row": place(3)}, device_id_type=MESH)

    pl.semaphore_wait(barrier, 5)


def gather_kernel(own_ref, out_ref, send_sem, recv_sem, keep_sem):
    planes, strip, _ = own_ref.shape
    greet()
    keep = pltpu.make_async_copy(own_ref, out_ref.at[:, pl.ds(OWN * strip, strip)], keep_sem)
    keep.start()

    def work(role):
        edges = EDGES[role]

        def edge(number, plane):
            source, half, target, slot = edges[number]
            if source == OWN:
                first = 0 if half < 2 else strip // 2
                origin = own_ref.at[plane, pl.ds(first, strip if half == 0 else strip // 2)]
            else:
                origin = out_ref.at[plane, rows_of(source, half, strip)]
            return pltpu.make_async_remote_copy(
                src_ref=origin,
                dst_ref=out_ref.at[plane, rows_of(slot, half, strip)],
                send_sem=send_sem.at[number, plane],
                recv_sem=recv_sem.at[slot, plane],
                device_id={"row": place(target)},
                device_id_type=MESH,
            )

        def arrived(slot, plane):
            back, _, half = ARRIVE[role][slot]
            spot = out_ref.at[plane, rows_of(slot, half, strip)]
            pltpu.make_async_remote_copy(
                src_ref=spot,
                dst_ref=spot,
                send_sem=send_sem.at[0, plane],
                recv_sem=recv_sem.at[slot, plane],
                device_id={"row": place(back)},
                device_id_type=MESH,
            ).wait_recv()

        near = P2 if role < 2 else M2
        far = {0: M1, 1: None, 2: P2, 3: P2}[role]

        def launch(source, plane):
            for number in range(len(edges)):
                if edges[number][0] == source:
                    edge(number, plane).start()

        for plane in range(planes):
            launch(OWN, plane)
        for step in range(planes + 1):
            if step < planes:
                arrived(near, step)
                launch(near, step)
            if step > 0 and far is not None:
                arrived(far, step - 1)
                launch(far, step - 1)
        for plane in range(planes):
            for slot in ARRIVE[role]:
                if slot not in (near, far):
                    arrived(slot, plane)
            for number in range(len(edges)):
                edge(number, plane).wait_send()

    me = lax.axis_index("row")
    for role in EDGES:
        pl.when(me % 4 == role)(functools.partial(work, role))
    keep.wait()


def scatter_kernel(grad_ref, out_ref, total, held, send_sem, recv_sem, load_sem):
    planes, strip = out_ref.shape[0], out_ref.shape[1]
    loads = [
        pltpu.make_async_copy(grad_ref.at[plane], total.at[plane], load_sem.at[plane])
        for plane in range(planes)
    ]
    for load in loads:
        load.start()
    greet()

    def work(role):
        edges = EDGES[role]
        slots = ARRIVE[role]

        def returned(slot, plane):
            target, number, half = slots[slot]
            count = strip if half == 0 else strip // 2
            return pltpu.make_async_remote_copy(
                src_ref=total.at[plane, rows_of(slot, half, strip)],
                dst_ref=held.at[number, plane, pl.ds(0, count)],
                send_sem=send_sem.at[slot, plane],
                recv_sem=recv_sem.at[number, plane],
                device_id={"row": place(target)},
                device_id_type=MESH,
            )

        def absorb(source, plane):
            for number, (origin, half, target, _) in enumerate(edges):
                if origin != source:
                    continue
                count = strip if half == 0 else strip // 2
                spot = held.at[number, plane, pl.ds(0, count)]
                pltpu.make_async_remote_copy(
                    src_ref=spot,
                    dst_ref=spot,
                    send_sem=send_sem.at[0, plane],
                    recv_sem=recv_sem.at[number, plane],
                    device_id={"row": place(target)},
                    device_id_type=MESH,
                ).wait_recv()
                rows = rows_of(source, half, strip)
                total[plane, rows] = total[plane, rows] + held[number, plane, pl.ds(0, count)]

        near = P2 if role < 2 else M2
        far = {0: M1, 1: None, 2: P2, 3: P2}[role]
        order = [slot for slot in (M2, P3, P1, M1) if slot in slots and slot not in (near, far)]
        for plane in range(planes):
            loads[plane].wait()
            for slot in order:
                returned(slot, plane).start()
        if far is not None:
            for plane in range(planes):
                absorb(far, plane)
                returned(far, plane).start()
        for plane in range(planes):
            absorb(near, plane)
            returned(near, plane).start()
        for plane in range(planes):
            absorb(OWN, plane)
            out_ref[plane] = total[plane, pl.ds(OWN * strip, strip)]
        for plane in range(planes):
            for slot in slots:
                returned(slot, plane).wait_send()

    me = lax.axis_index("row")
    for role in EDGES:
        pl.when(me % 4 == role)(functools.partial(work, role))


def extract_kernel(spot_ref, full_ref, out_ref):
    edge, columns = out_ref.shape[-1], full_ref.shape[-1]
    step = 64
    turn = (columns - spot_ref[1]) % columns
    past = spot_ref[0] % 8
    base = pl.multiple_of(spot_ref[0] - past, 8)

    @pl.loop(0, edge // step)
    def _(i):
        rows = full_ref[0, pl.ds(pl.multiple_of(base + i * step, 8), step + 8), :]
        rows = pltpu.roll(rows, (step + 8 - past) % (step + 8), 0)[:step]
        out_ref[0, pl.ds(i * step, step), :] = pltpu.roll(rows, turn, 1)[:, :edge]


def insert_kernel(spot_ref, grad_ref, out_ref, wide_ref):
    edge, columns = grad_ref.shape[-1], out_ref.shape[-1]
    step = 64
    past = spot_ref[0] % 8
    base = pl.multiple_of(spot_ref[0] - past, 8)
    out_ref[...] = jnp.zeros_like(out_ref)
    wide_ref[pl.ds(0, 8), :] = jnp.zeros((8, columns), jnp.float32)
    wide_ref[pl.ds(edge + 8, step), :] = jnp.zeros((step, columns), jnp.float32)

    @pl.loop(0, edge // step)
    def _(i):
        rows = grad_ref[0, pl.ds(i * step, step), :]
        wide = jnp.concatenate([rows, jnp.zeros((step, columns - edge), jnp.float32)], axis=1)
        wide_ref[pl.ds(i * step + 8, step), :] = pltpu.roll(wide, spot_ref[1], 1)

    @pl.loop(0, edge // step)
    def _(i):
        rows = wide_ref[pl.ds(i * step, step + 8), :]
        out_ref[0, pl.ds(pl.multiple_of(base + i * step, 8), step), :] = pltpu.roll(rows, step + past, 0)[:step]

    rows = wide_ref[pl.ds(edge, 16), :]
    out_ref[0, pl.ds(pl.multiple_of(base + edge, 8), 8), :] = pltpu.roll(rows, 8 + past, 0)[:8]


def gather(own, height):
    planes, strip, columns = own.shape
    return pl.pallas_call(
        gather_kernel,
        name="gather",
        out_shape=jax.ShapeDtypeStruct((planes, height, columns), jnp.float32),
        in_specs=[pl.BlockSpec(memory_space=pltpu.VMEM)],
        out_specs=pl.BlockSpec(memory_space=pl.ANY),
        scratch_shapes=[
            pltpu.SemaphoreType.DMA((MAX_EDGES, planes)),
            pltpu.SemaphoreType.DMA((6, planes)),
            pltpu.SemaphoreType.DMA,
        ],
        compiler_params=pltpu.CompilerParams(collective_id=0, has_side_effects=True),
    )(own)


def scatter(grads, strip):
    planes, height, columns = grads.shape
    return pl.pallas_call(
        scatter_kernel,
        name="scatter",
        out_shape=jax.ShapeDtypeStruct((planes, strip, columns), jnp.float32),
        in_specs=[pl.BlockSpec(memory_space=pl.ANY)],
        out_specs=pl.BlockSpec(memory_space=pltpu.VMEM),
        scratch_shapes=[
            pltpu.VMEM((planes, height, columns), jnp.float32),
            pltpu.VMEM((MAX_EDGES, planes, strip, columns), jnp.float32),
            pltpu.SemaphoreType.DMA((6, planes)),
            pltpu.SemaphoreType.DMA((MAX_EDGES, planes)),
            pltpu.SemaphoreType.DMA((planes,)),
        ],
        compiler_params=pltpu.CompilerParams(collective_id=1, has_side_effects=True),
    )(grads)


def local_move(kernel, name, spot, source, shape, scratch=()):
    planes = source.shape[0]
    return pl.pallas_call(
        kernel,
        name=name,
        out_shape=jax.ShapeDtypeStruct((planes, *shape), jnp.float32),
        grid_spec=pltpu.PrefetchScalarGridSpec(
            num_scalar_prefetch=1,
            grid=(planes,),
            in_specs=[pl.BlockSpec((1, *source.shape[1:]), lambda plane, spot: (plane, 0, 0))],
            out_specs=pl.BlockSpec((1, *shape), lambda plane, spot: (plane, 0, 0)),
            scratch_shapes=scratch,
        ),
    )(spot, source)


def dft_mats(length, flip):
    index = jnp.arange(length, dtype=jnp.int32)
    angles = (index[:, None] * index[None, :] % length).astype(jnp.float32) * (
        -2.0 * math.pi / length
    )
    factor = 1.0 / math.sqrt(length)
    cos_table = (jnp.cos(angles) * factor).astype(jnp.bfloat16)
    sin_table = (jnp.sin(angles) * factor).astype(jnp.bfloat16)
    if flip:
        sin_table = -sin_table
    left_real = jnp.concatenate([cos_table, -sin_table], axis=1)
    left_imag = jnp.concatenate([sin_table, cos_table], axis=1)
    right_real = jnp.concatenate([cos_table, -sin_table], axis=0)
    right_imag = jnp.concatenate([sin_table, cos_table], axis=0)
    return (left_real, left_imag, right_real, right_imag)


def transform(real_part, imag_part, mats):
    left_real, left_imag, right_real, right_imag = mats
    stacked = jnp.concatenate(
        [real_part.astype(jnp.bfloat16), imag_part.astype(jnp.bfloat16)], axis=0
    )
    half_real = jnp.dot(left_real, stacked, preferred_element_type=jnp.float32).astype(jnp.bfloat16)
    half_imag = jnp.dot(left_imag, stacked, preferred_element_type=jnp.float32).astype(jnp.bfloat16)
    joined = jnp.concatenate([half_real, half_imag], axis=1)
    return (
        jnp.dot(joined, right_real, preferred_element_type=jnp.float32),
        jnp.dot(joined, right_imag, preferred_element_type=jnp.float32),
    )


def cmul(a_real, a_imag, b_real, b_imag):
    return (a_real * b_real - a_imag * b_imag, a_real * b_imag + a_imag * b_real)


def cmul_conj(a_real, a_imag, b_real, b_imag):
    return (a_real * b_real + a_imag * b_imag, a_real * b_imag - a_imag * b_real)


def window_gradient(window, probe, amplitude, phase, forward, inverse):
    prop_real = jnp.cos(phase)
    prop_imag = jnp.sin(phase)
    probe_real, probe_imag = (probe[0], probe[1])
    first_real, first_imag = (window[0], window[1])
    second_real, second_imag = (window[2], window[3])
    exit_real, exit_imag = cmul(probe_real, probe_imag, first_real, first_imag)
    freq_real, freq_imag = transform(exit_real, exit_imag, forward)
    moved_real, moved_imag = cmul(freq_real, freq_imag, prop_real, prop_imag)
    inner_real, inner_imag = transform(moved_real, moved_imag, inverse)
    wave_real, wave_imag = cmul(inner_real, inner_imag, second_real, second_imag)
    far_real, far_imag = transform(wave_real, wave_imag, forward)
    modulus = jnp.sqrt(far_real * far_real + far_imag * far_imag)
    ratio = amplitude / jnp.maximum(modulus, 0.1)
    resid_real = far_real * (1.0 - ratio)
    resid_imag = far_imag * (1.0 - ratio)
    back_real, back_imag = transform(resid_real, resid_imag, inverse)
    grad2_real, grad2_imag = cmul_conj(inner_real, inner_imag, back_real, back_imag)
    mid_real, mid_imag = cmul_conj(second_real, second_imag, back_real, back_imag)
    spec_real, spec_imag = transform(mid_real, mid_imag, forward)
    unprop_real, unprop_imag = cmul_conj(prop_real, prop_imag, spec_real, spec_imag)
    entry_real, entry_imag = transform(unprop_real, unprop_imag, inverse)
    grad1_real, grad1_imag = cmul_conj(probe_real, probe_imag, entry_real, entry_imag)
    return jnp.stack([grad1_real, grad1_imag, grad2_real, grad2_imag])


def body(object_field, row_offset, col_offset, amplitudes, probe, phase):
    strip, columns = object_field.shape[2:]
    edge = probe.shape[1]
    half = strip // 2
    height = 5 * strip + half
    forward = dft_mats(edge, False)
    inverse = dft_mats(edge, True)
    own = object_field.reshape(4, strip, columns)
    spot = jnp.concatenate([row_offset + half, col_offset])
    around = gather(own, height)
    window = local_move(extract_kernel, "extract", spot, around, (edge, edge))
    grads = window_gradient(window, probe, amplitudes[0], phase, forward, inverse)
    spread = local_move(
        insert_kernel, "insert", spot, grads, (height, columns),
        [pltpu.VMEM((edge + 72, columns), jnp.float32)],
    )
    total = scatter(spread, strip)
    return (own - 0.5 * total).reshape(object_field.shape)


def solution(mesh):
    placed = (
        P(None, None, ("scan", "row"), None),
        P(("scan", "row")),
        P(("scan", "row")),
        P(("scan", "row"), None, None),
        P("scan", None, None),
        P(),
    )
    return jax.shard_map(
        body,
        mesh=mesh,
        in_specs=placed,
        out_specs=P(None, None, ("scan", "row"), None),
        check_vma=False,
    )
```

time: 253 us -> 176 us (0.70)
  Pallas kernels: 0 us -> 132 us
  waiting for transfers between devices: 90.6 us -> 0 us
  local copies, waits for them, and re-layouts: 77.7 us -> 6.26 us
  other arithmetic: 28.9 us -> 16.2 us
  starting transfers between devices: 11 us -> 0 us
  blocking collectives: 10.7 us -> 0 us
  between operations: 11.3 us -> 1.54 us
    pallas_call x0 -> x4, Pallas kernels: none -> 132 us  [the longest x1 60.2 us: scatter(): pl.pallas_call(scatter_kernel, name='scatter', out_shape=jax.ShapeDtypeSt...]
    ppermute x10 -> x0, waiting for transfers between devices: 90.6 us -> none  [shifted(): return lax.ppermute(block, axis, route)]
    dynamic_update_slice x7 -> x0, local copies, waits for them, and re-layouts: 46.7 us -> none  [the longest x6 33 us: add_into(): return lax.dynamic_update_slice(total, current + piece, spot)]
    add x5 -> x0, other arithmetic: 11.8 us -> none  [add_into(): return lax.dynamic_update_slice(total, current + piece, spot)]
    ppermute x10 -> x0, starting transfers between devices: 11 us -> none  [shifted(): return lax.ppermute(block, axis, route)]
    unnamed x1 -> x0, blocking collectives: 10.7 us -> none
    unnamed x15 -> x10, local copies, waits for them, and re-layouts: 10.3 us -> 2.41 us
    slice x2 -> x0, local copies, waits for them, and re-layouts: 6.53 us -> none  [body(): canvas[:, :, bounds[owner][0]:bounds[owner][1]]]
  transfers between devices with their start and end apart: 10 -> 0, of which waited for: 4 -> 0; matrix products, arithmetic and copies ran while one was open for 23% -> 0% of each run, Pallas kernels for 0% -> 0%
where the time goes in v1:
time: 176 us; the launch traced here: 175 us
  Pallas kernels  132 us (75%)
  matrix products  19.5 us (11%)
  other arithmetic  16.2 us (9%)
  local copies, waits for them, and re-layouts  6.26 us (4%)
    pallas_call x1, Pallas kernels, scatter(): pl.pallas_call(scatter_kernel, name='scatter', out_shape=jax.ShapeDtypeSt...  60.2 us
    pallas_call x1, Pallas kernels, gather(): pl.pallas_call(gather_kernel, name='gather', out_shape=jax.ShapeDtypeStru...  51.8 us
    pallas_call x2, Pallas kernels, local_move(): pl.pallas_call(kernel, name=name, out_shape=jax.ShapeDtypeStruct((planes,...  19.5 us
    dot_general x6, matrix products, transform(): jnp.dot(joined, right_real, preferred_element_type=jnp.float32)  5.45 us
    dot_general x6, matrix products, transform(): jnp.dot(joined, right_imag, preferred_element_type=jnp.float32)  4.82 us
    dot_general x6, matrix products, transform(): jnp.dot(left_imag, stacked, preferred_element_type=jnp.float32)  4.74 us
    dot_general x6, matrix products, transform(): jnp.dot(left_real, stacked, preferred_element_type=jnp.float32)  4.5 us
    convert_element_type x1, other arithmetic, dft_mats(): sin_table = (jnp.sin(angles) * factor).astype(jnp.bfloat16)  4.39 us

profile of v1, /device:TPU:1, one launch (start us, length us, event | category | flops | bytes accessed | tf_op | source)
XLA Modules:
  0.0 175.1 jit_solution(3780846169762852520)
XLA Ops:
  0.0 4.4 %multiply_convert_fusion.2 = (bf16[512,512]{1,0:T(8,128)(2,1)S(1)}, bf16[512,512]{1,0:T(8,128)(2,1)S(1)}) fusion(), kind=kLoop, calls=%fused_computation.74 | loop fusion | flops 4718592 | bytes 1048576 | tf_op jit(solution)/shard_map/convert_element_type | solution.py:320
  6.3 51.8 %gather.1.full_ref = f32[4,704,768]{2,1,0:T(8,128)} custom-call(f32[4,128,768]{2,1,0:T(8,128)} %bitcast.85), custom_call_target="tpu_custom_call" | custom-call | tf_op jit(solution)/shard_map/gather/pallas_call | solution.py:263
  58.1 9.1 %extract.1 = f32[4,512,512]{2,1,0:T(8,128)} custom-call(s32[2]{0:T(128)} %pad_add_fusion.spot_ref, f32[4,704,768]{2,1,0:T(8,128)} %gather.1.full_ref), custom_call_target="tpu_custom_call" | custom-call | tf_op jit(solution)/shard_map/extract/pallas_call | solution.py:299
  67.2 2.1 %fusion.5 = (bf16[512,512]{1,0:T(8,128)(2,1)S(1)}, bf16[512,512]{1,0:T(8,128)(2,1)S(1)}) fusion(f32[4,512,512]{2,1,0:T(8,128)} %extract.1, f32[2,512,512]{2,1,0:T(8,128)S(1)} %copy-done.2), kind=kLoop, calls=%fused_computation.51 | loop fusion | flops 2097152 | bytes 5242880 | tf_op jit(solution)/shard_map/convert_element_type | solution.py:333
  69.3 0.8 convolution_convert_fusion.10
  70.0 4.0 %fusion.27 = bf16[512,512]{1,0:T(8,128)(2,1)S(1)} fusion(), kind=kLoop, calls=%fused_computation.91 | loop fusion | flops 4980736 | bytes 524288 | tf_op jit(solution)/shard_map/neg | solution.py:322
  74.1 0.8 convolution_convert_fusion.11
  76.0 3.9 %fusion.52 = (f32[512,512]{1,0:T(8,128)S(1)}, f32[512,512]{1,0:T(8,128)S(1)}) fusion(f32[512,512]{1,0:T(8,128)S(1)} %copy-done.3), kind=kLoop, calls=%fused_computation.117 | loop fusion | bytes 3145728 | tf_op jit(solution)/shard_map/sin | solution.py:354
  79.9 0.9 subtract_convert_fusion.3
  81.5 0.8 convolution_convert_fusion.8
  83.1 1.4 copy-done
  84.5 0.9 subtract_convert_fusion.2
  88.1 1.2 multiply_convert_fusion.1
  89.3 0.7 convolution_convert_fusion.5
  90.1 0.8 convolution_convert_fusion.4
  91.6 1.1 add_convert_fusion.1
  93.5 0.8 convolution_convert_fusion.2
  95.0 0.9 add_convert_fusion
  96.6 1.0 convolution_convert_fusion
  98.3 0.9 fusion.9
  99.3 2.5 %pad_maximum_fusion.grad_ref = f32[4,512,512]{2,1,0:T(8,128)} fusion(f32[1,512,512]{2,1,0:T(8,128)S(1)} %get-tuple-element.21, f32[1,512,512]{2,1,0:T(8,128)S(1)} %get-tuple-element.22, f32[1,512,512]{2,1,0:T(8,128)S(1)} %get-tuple-element.12, f32[1,512,512]{2,1,0:T(8,128)S(1)} %get-tuple-element.11), kind=kLoop, calls=%fused_computation | loop fusion | flops 3145728 | bytes 8388608 | tf_op jit(solution)/shard_map/stack | solution.py:375
  101.7 10.5 %insert.1.grad_ref = f32[4,704,768]{2,1,0:T(8,128)} custom-call(s32[2]{0:T(128)} %pad_add_fusion.spot_ref, f32[4,512,512]{2,1,0:T(8,128)} %pad_maximum_fusion.grad_ref), custom_call_target="tpu_custom_call" | custom-call | tf_op jit(solution)/shard_map/insert/pallas_call | solution.py:299
  112.2 60.2 %scatter.1 = f32[4,128,768]{2,1,0:T(8,128)} custom-call(f32[4,704,768]{2,1,0:T(8,128)} %insert.1.grad_ref), custom_call_target="tpu_custom_call" | custom-call | tf_op jit(solution)/shard_map/scatter/pallas_call | solution.py:280
  172.4 2.7 %multiply_subtract_fusion = f32[4,128,768]{2,1,0:T(8,128)} fusion(f32[4,128,768]{2,1,0:T(8,128)} %scatter.1, f32[2,2,128,768]{3,2,1,0:T(8,128)S(1)} %copy-done.1), kind=kLoop, calls=%fused_computation.1 | loop fusion | flops 786432 | bytes 4718592 | tf_op jit(solution)/shard_map/sub | solution.py:395
  (21 shorter events, 9.7 us)
Async XLA Ops:
  58.1 9.1 %copy-start.2 = (f32[2,512,512]{2,1,0:T(8,128)S(1)}, f32[2,512,512]{2,1,0:T(8,128)}, u32[]{:S(2)}) copy-start(f32[2,512,512]{2,1,0:T(8,128)} %param.10) | copy-start | bytes 6291460
  74.8 1.2 copy-start.3
  82.3 2.2 %copy-start = (f32[4,512,512]{2,1,0:T(8,128)S(1)}, f32[4,512,512]{2,1,0:T(8,128)}, u32[]{:S(2)}) copy-start(f32[4,512,512]{2,1,0:T(8,128)} %extract.1) | copy-start | bytes 12582916
  86.9 1.2 copy-start.4
  112.2 60.2 %copy-start.1 = (f32[2,2,128,768]{3,2,1,0:T(8,128)S(1)}, f32[2,2,128,768]{3,2,1,0:T(8,128)}, u32[]{:S(2)}) copy-start(f32[2,2,128,768]{3,2,1,0:T(8,128)} %param.6) | copy-start | bytes 4718596

commit v2 on v1

--- a/solution.py
+++ b/solution.py
@@ -13,22 +13,29 @@
 M2, M1, OWN, P1, P2, P3 = range(6)
 EDGES = {
     0: (
-        (OWN, 0, "y", M2), (OWN, 1, -3, P3), (OWN, 0, "c", M1),
+        (OWN, 2, "y", M2), (OWN, 1, -3, P3), (OWN, 0, "c", M1),
         (P2, 2, 4, M2), (P2, 0, "c", P1), (M1, 2, "c", M2),
     ),
     1: (
         (OWN, 0, "y", M2), (OWN, 0, "c", P1),
-        (P2, 0, 3, M1), (P2, 1, "c", P3),
+        (P2, 0, 3, M1), (P2, 1, "c", P3), (P3, 1, "y", P1),
     ),
     2: (
         (OWN, 0, "y", P2), (OWN, 1, -3, P3), (OWN, 0, "c", M1),
-        (M2, 0, -4, P2), (P2, 0, "c", P1),
+        (M2, 2, -4, P2), (P2, 2, "c", P1),
     ),
     3: (
         (OWN, 0, "y", P2), (OWN, 0, "c", P1),
-        (M2, 0, -4, P2), (M2, 0, "c", M1), (P2, 1, "c", P3),
+        (M2, 0, -4, P2), (M2, 0, "c", M1), (P2, 1, "c", P3), (P1, 1, "c", P2),
     ),
 }
+RELAYS = {
+    0: ((P2, 0), (M1, 0)),
+    1: ((P2, 0), (P3, 1)),
+    2: ((M2, 2), (P2, 2)),
+    3: ((M2, 0), (P1, 1), (P2, 0)),
+}
+COLUMN_PARTS = 2
 BACK = {"y": "y", "c": "c", 3: -3, -3: 3, 4: -4, -4: 4}
 MAX_EDGES = max(len(edges) for edges in EDGES.values())
 
@@ -45,7 +52,7 @@
     table = {role: {} for role in EDGES}
     for role, edges in EDGES.items():
         for number, (source, half, target, slot) in enumerate(edges):
-            table[role_at(role, target)][slot] = (BACK[target], number, half)
+            table[role_at(role, target)][slot, half] = (BACK[target], number)
     return table
 
 
@@ -67,6 +74,19 @@
     return pl.ds(slot * strip + (half - 1) * (strip // 2), strip // 2)
 
 
+def mark(key):
+    return 2 * key[0] + (key[1] == 2)
+
+
+def source_key(role, source, half):
+    return (source, 0) if (source, 0) in ARRIVE[role] else (source, half)
+
+
+def chunks_of(planes, columns):
+    width = columns // COLUMN_PARTS
+    return [(plane, pl.ds(part * width, width)) for plane in range(planes) for part in range(COLUMN_PARTS)]
+
+
 def greet():
     me = lax.axis_index("row")
     barrier = pltpu.get_barrier_semaphore()
@@ -85,7 +105,8 @@
 
 
 def gather_kernel(own_ref, out_ref, send_sem, recv_sem, keep_sem):
-    planes, strip, _ = own_ref.shape
+    planes, strip, columns = own_ref.shape
+    chunks = chunks_of(planes, columns)
     greet()
     keep = pltpu.make_async_copy(own_ref, out_ref.at[:, pl.ds(OWN * strip, strip)], keep_sem)
     keep.start()
@@ -93,57 +114,54 @@
     def work(role):
         edges = EDGES[role]
 
-        def edge(number, plane):
+        def edge(number, chunk):
             source, half, target, slot = edges[number]
+            plane, lanes = chunks[chunk]
             if source == OWN:
-                first = 0 if half < 2 else strip // 2
-                origin = own_ref.at[plane, pl.ds(first, strip if half == 0 else strip // 2)]
+                origin = own_ref.at[plane, rows_of(0, half, strip), lanes]
             else:
-                origin = out_ref.at[plane, rows_of(source, half, strip)]
+                origin = out_ref.at[plane, rows_of(source, half, strip), lanes]
             return pltpu.make_async_remote_copy(
                 src_ref=origin,
-                dst_ref=out_ref.at[plane, rows_of(slot, half, strip)],
-                send_sem=send_sem.at[number, plane],
-                recv_sem=recv_sem.at[slot, plane],
+                dst_ref=out_ref.at[plane, rows_of(slot, half, strip), lanes],
+                send_sem=send_sem.at[number, chunk],
+                recv_sem=recv_sem.at[mark((slot, half)), chunk],
                 device_id={"row": place(target)},
                 device_id_type=MESH,
             )
 
-        def arrived(slot, plane):
-            back, _, half = ARRIVE[role][slot]
-            spot = out_ref.at[plane, rows_of(slot, half, strip)]
+        def arrived(key, chunk):
+            back, _ = ARRIVE[role][key]
+            plane, lanes = chunks[chunk]
+            spot = out_ref.at[plane, rows_of(*key, strip), lanes]
             pltpu.make_async_remote_copy(
                 src_ref=spot,
                 dst_ref=spot,
-                send_sem=send_sem.at[0, plane],
-                recv_sem=recv_sem.at[slot, plane],
+                send_sem=send_sem.at[0, chunk],
+                recv_sem=recv_sem.at[mark(key), chunk],
                 device_id={"row": place(back)},
                 device_id_type=MESH,
             ).wait_recv()
 
-        near = P2 if role < 2 else M2
-        far = {0: M1, 1: None, 2: P2, 3: P2}[role]
-
-        def launch(source, plane):
+        def launch(key, chunk):
+            for number, (source, half, _, _) in enumerate(edges):
+                if (source == OWN) if key is None else (source != OWN and source_key(role, source, half) == key):
+                    edge(number, chunk).start()
+
+        for chunk in range(len(chunks)):
+            launch(None, chunk)
+        relays = RELAYS[role]
+        for step in range(len(chunks) + len(relays) - 1):
+            for late, key in enumerate(relays):
+                if 0 <= step - late < len(chunks):
+                    arrived(key, step - late)
+                    launch(key, step - late)
+        for chunk in range(len(chunks)):
+            for key in ARRIVE[role]:
+                if key not in relays:
+                    arrived(key, chunk)
             for number in range(len(edges)):
-                if edges[number][0] == source:
-                    edge(number, plane).start()
-
-        for plane in range(planes):
-            launch(OWN, plane)
-        for step in range(planes + 1):
-            if step < planes:
-                arrived(near, step)
-                launch(near, step)
-            if step > 0 and far is not None:
-                arrived(far, step - 1)
-                launch(far, step - 1)
-        for plane in range(planes):
-            for slot in ARRIVE[role]:
-                if slot not in (near, far):
-                    arrived(slot, plane)
-            for number in range(len(edges)):
-                edge(number, plane).wait_send()
+                edge(number, chunk).wait_send()
 
     me = lax.axis_index("row")
     for role in EDGES:
@@ -152,7 +170,8 @@
 
 
 def scatter_kernel(grad_ref, out_ref, total, held, send_sem, recv_sem, load_sem):
-    planes, strip = out_ref.shape[0], out_ref.shape[1]
+    planes, strip, columns = out_ref.shape
+    chunks = chunks_of(planes, columns)
     loads = [
         pltpu.make_async_copy(grad_ref.at[plane], total.at[plane], load_sem.at[plane])
         for plane in range(planes)
@@ -163,57 +182,59 @@
 
     def work(role):
         edges = EDGES[role]
-        slots = ARRIVE[role]
-
-        def returned(slot, plane):
-            target, number, half = slots[slot]
-            count = strip if half == 0 else strip // 2
+        keys = ARRIVE[role]
+
+        def returned(key, chunk):
+            target, number = keys[key]
+            plane, lanes = chunks[chunk]
+            count = strip if key[1] == 0 else strip // 2
             return pltpu.make_async_remote_copy(
-                src_ref=total.at[plane, rows_of(slot, half, strip)],
-                dst_ref=held.at[number, plane, pl.ds(0, count)],
-                send_sem=send_sem.at[slot, plane],
-                recv_sem=recv_sem.at[number, plane],
+                src_ref=total.at[plane, rows_of(*key, strip), lanes],
+                dst_ref=held.at[number, plane, pl.ds(0, count), lanes],
+                send_sem=send_sem.at[mark(key), chunk],
+                recv_sem=recv_sem.at[number, chunk],
                 device_id={"row": place(target)},
                 device_id_type=MESH,
             )
 
-        def absorb(source, plane):
-            for number, (origin, half, target, _) in enumerate(edges):
-                if origin != source:
+        def absorb(key, chunk):
+            plane, lanes = chunks[chunk]
+            for number, (source, half, target, _) in enumerate(edges):
+                if not ((source == OWN) if key is None else (source != OWN and source_key(role, source, half) == key)):
                     continue
                 count = strip if half == 0 else strip // 2
-                spot = held.at[number, plane, pl.ds(0, count)]
+                spot = held.at[number, plane, pl.ds(0, count), lanes]
                 pltpu.make_async_remote_copy(
                     src_ref=spot,
                     dst_ref=spot,
-                    send_sem=send_sem.at[0, plane],
-                    recv_sem=recv_sem.at[number, plane],
+                    send_sem=send_sem.at[0, chunk],
+                    recv_sem=recv_sem.at[number, chunk],
                     device_id={"row": place(target)},
                     device_id_type=MESH,
                 ).wait_recv()
                 rows = rows_of(source, half, strip)
-                total[plane, rows] = total[plane, rows] + held[number, plane, pl.ds(0, count)]
-
-        near = P2 if role < 2 else M2
-        far = {0: M1, 1: None, 2: P2, 3: P2}[role]
-        order = [slot for slot in (M2, P3, P1, M1) if slot in slots and slot not in (near, far)]
-        for plane in range(planes):
-            loads[plane].wait()
-            for slot in order:
-                returned(slot, plane).start()
-        if far is not None:
-            for plane in range(planes):
-                absorb(far, plane)
-                returned(far, plane).start()
-        for plane in range(planes):
-            absorb(near, plane)
-            returned(near, plane).start()
-        for plane in range(planes):
-            absorb(OWN, plane)
-            out_ref[plane] = total[plane, pl.ds(OWN * strip, strip)]
-        for plane in range(planes):
-            for slot in slots:
-                returned(slot, plane).wait_send()
+                total[plane, rows, lanes] = total[plane, rows, lanes] + held[number, plane, pl.ds(0, count), lanes]
+
+        relays = RELAYS[role][::-1]
+        order = [key for key in keys if key not in relays]
+        order.sort(key=lambda key: (keys[key][0] == "c" and key[0] == M1, key[0]))
+        for chunk in range(len(chunks)):
+            if chunk % COLUMN_PARTS == 0:
+                loads[chunks[chunk][0]].wait()
+            for key in order:
+                returned(key, chunk).start()
+        for step in range(len(chunks) + len(relays) - 1):
+            for late, key in enumerate(relays):
+                if 0 <= step - late < len(chunks):
+                    absorb(key, step - late)
+                    returned(key, step - late).start()
+        for chunk in range(len(chunks)):
+            plane, lanes = chunks[chunk]
+            absorb(None, chunk)
+            out_ref[plane, :, lanes] = total[plane, pl.ds(OWN * strip, strip), lanes]
+        for chunk in range(len(chunks)):
+            for key in keys:
+                returned(key, chunk).wait_send()
 
     me = lax.axis_index("row")
     for role in EDGES:
@@ -267,8 +288,8 @@
         in_specs=[pl.BlockSpec(memory_space=pltpu.VMEM)],
         out_specs=pl.BlockSpec(memory_space=pl.ANY),
         scratch_shapes=[
-            pltpu.SemaphoreType.DMA((MAX_EDGES, planes)),
-            pltpu.SemaphoreType.DMA((6, planes)),
+            pltpu.SemaphoreType.DMA((MAX_EDGES, planes * COLUMN_PARTS)),
+            pltpu.SemaphoreType.DMA((12, planes * COLUMN_PARTS)),
             pltpu.SemaphoreType.DMA,
         ],
         compiler_params=pltpu.CompilerParams(collective_id=0, has_side_effects=True),
@@ -286,8 +307,8 @@
         scratch_shapes=[
             pltpu.VMEM((planes, height, columns), jnp.float32),
             pltpu.VMEM((MAX_EDGES, planes, strip, columns), jnp.float32),
-            pltpu.SemaphoreType.DMA((6, planes)),
-            pltpu.SemaphoreType.DMA((MAX_EDGES, planes)),
+            pltpu.SemaphoreType.DMA((12, planes * COLUMN_PARTS)),
+            pltpu.SemaphoreType.DMA((MAX_EDGES, planes * COLUMN_PARTS)),
             pltpu.SemaphoreType.DMA((planes,)),
         ],
         compiler_params=pltpu.CompilerParams(collective_id=1, has_side_effects=True),

time: 176 us -> 167 us (0.949)
  Pallas kernels: 132 us -> 123 us
    pallas_call x1, Pallas kernels: 60.2 us -> 54.7 us  [scatter(): pl.pallas_call(scatter_kernel, name='scatter', out_shape=jax.ShapeDtypeSt...]
    pallas_call x1, Pallas kernels: 51.8 us -> 49.2 us  [gather(): pl.pallas_call(gather_kernel, name='gather', out_shape=jax.ShapeDtypeStru...]
where the time goes in v2:
time: 167 us
  Pallas kernels  123 us (74%)
  matrix products  19.5 us (12%)
  other arithmetic  16.2 us (10%)
  local copies, waits for them, and re-layouts  6.26 us (4%)
    pallas_call x1, Pallas kernels, scatter(): pl.pallas_call(scatter_kernel, name='scatter', out_shape=jax.ShapeDtypeSt...  54.7 us
    pallas_call x1, Pallas kernels, gather(): pl.pallas_call(gather_kernel, name='gather', out_shape=jax.ShapeDtypeStru...  49.2 us
    pallas_call x2, Pallas kernels, local_move(): pl.pallas_call(kernel, name=name, out_shape=jax.ShapeDtypeStruct((planes,...  19.5 us
    dot_general x6, matrix products, transform(): jnp.dot(joined, right_real, preferred_element_type=jnp.float32)  5.45 us
    dot_general x6, matrix products, transform(): jnp.dot(joined, right_imag, preferred_element_type=jnp.float32)  4.83 us
    dot_general x6, matrix products, transform(): jnp.dot(left_imag, stacked, preferred_element_type=jnp.float32)  4.74 us
    dot_general x6, matrix products, transform(): jnp.dot(left_real, stacked, preferred_element_type=jnp.float32)  4.5 us
    convert_element_type x1, other arithmetic, dft_mats(): sin_table = (jnp.sin(angles) * factor).astype(jnp.bfloat16)  4.39 us

profile of v2, /device:TPU:1, one launch (start us, length us, event | category | flops | bytes accessed | tf_op | source)
XLA Modules:
  0.0 166.9 jit_solution(7670301309909531627)
XLA Ops:
  0.0 4.4 %multiply_convert_fusion.2 = (bf16[512,512]{1,0:T(8,128)(2,1)S(1)}, bf16[512,512]{1,0:T(8,128)(2,1)S(1)}) fusion(), kind=kLoop, calls=%fused_computation.74 | loop fusion | flops 4718592 | bytes 1048576 | tf_op jit(solution)/shard_map/convert_element_type | solution.py:341
  6.3 49.2 %gather.1.full_ref = f32[4,704,768]{2,1,0:T(8,128)} custom-call(f32[4,128,768]{2,1,0:T(8,128)} %bitcast.85), custom_call_target="tpu_custom_call" | custom-call | tf_op jit(solution)/shard_map/gather/pallas_call | solution.py:284
  55.5 9.1 %extract.1 = f32[4,512,512]{2,1,0:T(8,128)} custom-call(s32[2]{0:T(128)} %pad_add_fusion.spot_ref, f32[4,704,768]{2,1,0:T(8,128)} %gather.1.full_ref), custom_call_target="tpu_custom_call" | custom-call | tf_op jit(solution)/shard_map/extract/pallas_call | solution.py:320
  64.5 2.1 %fusion.5 = (bf16[512,512]{1,0:T(8,128)(2,1)S(1)}, bf16[512,512]{1,0:T(8,128)(2,1)S(1)}) fusion(f32[4,512,512]{2,1,0:T(8,128)} %extract.1, f32[2,512,512]{2,1,0:T(8,128)S(1)} %copy-done.2), kind=kLoop, calls=%fused_computation.51 | loop fusion | flops 2097152 | bytes 5242880 | tf_op jit(solution)/shard_map/convert_element_type | solution.py:354
  66.6 0.8 convolution_convert_fusion.10
  67.4 4.0 %fusion.27 = bf16[512,512]{1,0:T(8,128)(2,1)S(1)} fusion(), kind=kLoop, calls=%fused_computation.91 | loop fusion | flops 4980736 | bytes 524288 | tf_op jit(solution)/shard_map/neg | solution.py:343
  71.4 0.8 convolution_convert_fusion.11
  73.4 3.9 %fusion.52 = (f32[512,512]{1,0:T(8,128)S(1)}, f32[512,512]{1,0:T(8,128)S(1)}) fusion(f32[512,512]{1,0:T(8,128)S(1)} %copy-done.3), kind=kLoop, calls=%fused_computation.117 | loop fusion | bytes 3145728 | tf_op jit(solution)/shard_map/sin | solution.py:375
  77.2 0.9 subtract_convert_fusion.3
  78.1 0.7 convolution_convert_fusion.9
  78.9 0.8 convolution_convert_fusion.8
  80.4 1.4 copy-done
  81.8 0.9 subtract_convert_fusion.2
  85.5 1.2 multiply_convert_fusion.1
  86.7 0.7 convolution_convert_fusion.5
  87.4 0.8 convolution_convert_fusion.4
  88.9 1.1 add_convert_fusion.1
  92.3 0.9 add_convert_fusion
  94.0 1.0 convolution_convert_fusion
  95.7 0.9 fusion.9
  96.6 2.5 %pad_maximum_fusion.grad_ref = f32[4,512,512]{2,1,0:T(8,128)} fusion(f32[1,512,512]{2,1,0:T(8,128)S(1)} %get-tuple-element.21, f32[1,512,512]{2,1,0:T(8,128)S(1)} %get-tuple-element.22, f32[1,512,512]{2,1,0:T(8,128)S(1)} %get-tuple-element.12, f32[1,512,512]{2,1,0:T(8,128)S(1)} %get-tuple-element.11), kind=kLoop, calls=%fused_computation | loop fusion | flops 3145728 | bytes 8388608 | tf_op jit(solution)/shard_map/stack | solution.py:396
  99.1 10.5 %insert.1.grad_ref = f32[4,704,768]{2,1,0:T(8,128)} custom-call(s32[2]{0:T(128)} %pad_add_fusion.spot_ref, f32[4,512,512]{2,1,0:T(8,128)} %pad_maximum_fusion.grad_ref), custom_call_target="tpu_custom_call" | custom-call | tf_op jit(solution)/shard_map/insert/pallas_call | solution.py:320
  109.5 54.7 %scatter.1 = f32[4,128,768]{2,1,0:T(8,128)} custom-call(f32[4,704,768]{2,1,0:T(8,128)} %insert.1.grad_ref), custom_call_target="tpu_custom_call" | custom-call | tf_op jit(solution)/shard_map/scatter/pallas_call | solution.py:301
  164.2 2.7 %multiply_subtract_fusion = f32[4,128,768]{2,1,0:T(8,128)} fusion(f32[4,128,768]{2,1,0:T(8,128)} %scatter.1, f32[2,2,128,768]{3,2,1,0:T(8,128)S(1)} %copy-done.1), kind=kLoop, calls=%fused_computation.1 | loop fusion | flops 786432 | bytes 4718592 | tf_op jit(solution)/shard_map/sub | solution.py:416
  (21 shorter events, 9.7 us)
Async XLA Ops:
  55.4 9.1 %copy-start.2 = (f32[2,512,512]{2,1,0:T(8,128)S(1)}, f32[2,512,512]{2,1,0:T(8,128)}, u32[]{:S(2)}) copy-start(f32[2,512,512]{2,1,0:T(8,128)} %param.10) | copy-start | bytes 6291460
  72.2 1.2 copy-start.3
  79.6 2.2 %copy-start = (f32[4,512,512]{2,1,0:T(8,128)S(1)}, f32[4,512,512]{2,1,0:T(8,128)}, u32[]{:S(2)}) copy-start(f32[4,512,512]{2,1,0:T(8,128)} %extract.1) | copy-start | bytes 12582916
  84.2 1.2 copy-start.4
  109.5 54.7 %copy-start.1 = (f32[2,2,128,768]{3,2,1,0:T(8,128)S(1)}, f32[2,2,128,768]{3,2,1,0:T(8,128)}, u32[]{:S(2)}) copy-start(f32[2,2,128,768]{3,2,1,0:T(8,128)} %param.6) | copy-start | bytes 4718596

commit v3 on v2

--- a/solution.py
+++ b/solution.py
@@ -104,69 +104,140 @@
     pl.semaphore_wait(barrier, 5)
 
 
-def gather_kernel(own_ref, out_ref, send_sem, recv_sem, keep_sem):
+def table_rows(first, count, phase_ref, tables):
+    fore_left_real, fore_left_imag, fore_right_real, fore_right_imag = tables[0:4]
+    back_left_real, back_left_imag, back_right_real, back_right_imag = tables[4:8]
+    prop_real, prop_imag = tables[8:10]
+    edge = phase_ref.shape[0]
+    step = 16
+
+    @pl.loop(0, count // step)
+    def _(i):
+        start = pl.multiple_of(first + i * step, step)
+        rows, low, high = pl.ds(start, step), pl.ds(0, edge), pl.ds(edge, edge)
+        more = pl.ds(pl.multiple_of(edge + start, step), step)
+        line = lax.broadcasted_iota(jnp.int32, (step, edge), 0) + start
+        index = line * lax.broadcasted_iota(jnp.int32, (step, edge), 1)
+        wrapped = index & (edge - 1) if edge & (edge - 1) == 0 else lax.rem(index, edge)
+        angles = wrapped.astype(jnp.float32) * (-2.0 * math.pi / edge)
+        factor = 1.0 / math.sqrt(edge)
+        cosine = (jnp.cos(angles) * factor).astype(jnp.bfloat16)
+        plain = jnp.sin(angles) * factor
+        sine, minus = plain.astype(jnp.bfloat16), (-plain).astype(jnp.bfloat16)
+        fore_left_real[rows, low] = cosine
+        fore_left_real[rows, high] = minus
+        fore_left_imag[rows, low] = sine
+        fore_left_imag[rows, high] = cosine
+        fore_right_real[rows, :] = cosine
+        fore_right_real[more, :] = minus
+        fore_right_imag[rows, :] = sine
+        fore_right_imag[more, :] = cosine
+        back_left_real[rows, low] = cosine
+        back_left_real[rows, high] = sine
+        back_left_imag[rows, low] = minus
+        back_left_imag[rows, high] = cosine
+        back_right_real[rows, :] = cosine
+        back_right_real[more, :] = sine
+        back_right_imag[rows, :] = minus
+        back_right_imag[more, :] = cosine
+        prop_real[rows, :] = jnp.cos(phase_ref[rows, :])
+        prop_imag[rows, :] = jnp.sin(phase_ref[rows, :])
+
+
+def feeds(role, edge, key):
+    source, half = edge[0], edge[1]
+    if key is None:
+        return source == OWN
+    return source != OWN and source_key(role, source, half) == key
+
+
+def gather_kernel(own_ref, phase_ref, out_ref, *refs):
+    tables = refs[:10]
+    send_sem, recv_sem, keep_sem = refs[10:]
+    full = [out_ref.at[plane] for plane in range(own_ref.shape[0])]
     planes, strip, columns = own_ref.shape
     chunks = chunks_of(planes, columns)
+    me = lax.axis_index("row")
     greet()
-    keep = pltpu.make_async_copy(own_ref, out_ref.at[:, pl.ds(OWN * strip, strip)], keep_sem)
-    keep.start()
-
-    def work(role):
-        edges = EDGES[role]
-
-        def edge(number, chunk):
-            source, half, target, slot = edges[number]
-            plane, lanes = chunks[chunk]
-            if source == OWN:
-                origin = own_ref.at[plane, rows_of(0, half, strip), lanes]
-            else:
-                origin = out_ref.at[plane, rows_of(source, half, strip), lanes]
-            return pltpu.make_async_remote_copy(
-                src_ref=origin,
-                dst_ref=out_ref.at[plane, rows_of(slot, half, strip), lanes],
-                send_sem=send_sem.at[number, chunk],
-                recv_sem=recv_sem.at[mark((slot, half)), chunk],
-                device_id={"row": place(target)},
-                device_id_type=MESH,
-            )
-
-        def arrived(key, chunk):
-            back, _ = ARRIVE[role][key]
-            plane, lanes = chunks[chunk]
-            spot = out_ref.at[plane, rows_of(*key, strip), lanes]
-            pltpu.make_async_remote_copy(
-                src_ref=spot,
-                dst_ref=spot,
-                send_sem=send_sem.at[0, chunk],
-                recv_sem=recv_sem.at[mark(key), chunk],
-                device_id={"row": place(back)},
-                device_id_type=MESH,
-            ).wait_recv()
-
-        def launch(key, chunk):
-            for number, (source, half, _, _) in enumerate(edges):
-                if (source == OWN) if key is None else (source != OWN and source_key(role, source, half) == key):
-                    edge(number, chunk).start()
-
+
+    def edge(role, number, chunk):
+        source, half, target, slot = EDGES[role][number]
+        plane, lanes = chunks[chunk]
+        if source == OWN:
+            origin = own_ref.at[plane, rows_of(0, half, strip), lanes]
+        else:
+            origin = full[plane].at[rows_of(source, half, strip), lanes]
+        return pltpu.make_async_remote_copy(
+            src_ref=origin,
+            dst_ref=full[plane].at[rows_of(slot, half, strip), lanes],
+            send_sem=send_sem.at[number, chunk],
+            recv_sem=recv_sem.at[mark((slot, half)), chunk],
+            device_id={"row": place(target)},
+            device_id_type=MESH,
+        )
+
+    def arrived(role, key, chunk):
+        back, _ = ARRIVE[role][key]
+        plane, lanes = chunks[chunk]
+        spot = full[plane].at[rows_of(*key, strip), lanes]
+        pltpu.make_async_remote_copy(
+            src_ref=spot,
+            dst_ref=spot,
+            send_sem=send_sem.at[0, chunk],
+            recv_sem=recv_sem.at[mark(key), chunk],
+            device_id={"row": place(back)},
+            device_id_type=MESH,
+        ).wait_recv()
+
+    def launch(role, key, chunk):
+        for number, entry in enumerate(EDGES[role]):
+            if feeds(role, entry, key):
+                edge(role, number, chunk).start()
+
+    def begin(role):
         for chunk in range(len(chunks)):
-            launch(None, chunk)
-        relays = RELAYS[role]
-        for step in range(len(chunks) + len(relays) - 1):
-            for late, key in enumerate(relays):
-                if 0 <= step - late < len(chunks):
-                    arrived(key, step - late)
-                    launch(key, step - late)
+            launch(role, None, chunk)
+
+    def relay(role, step):
+        for late, key in enumerate(RELAYS[role]):
+            if 0 <= step - late < len(chunks):
+                arrived(role, key, step - late)
+                launch(role, key, step - late)
+
+    def rest(role, plane):
+        for chunk in range(plane * COLUMN_PARTS, (plane + 1) * COLUMN_PARTS):
+            for key in ARRIVE[role]:
+                if key not in RELAYS[role]:
+                    arrived(role, key, chunk)
+
+    def drain(role):
         for chunk in range(len(chunks)):
-            for key in ARRIVE[role]:
-                if key not in relays:
-                    arrived(key, chunk)
-            for number in range(len(edges)):
-                edge(number, chunk).wait_send()
-
-    me = lax.axis_index("row")
-    for role in EDGES:
-        pl.when(me % 4 == role)(functools.partial(work, role))
-    keep.wait()
+            for number in range(len(EDGES[role])):
+                edge(role, number, chunk).wait_send()
+
+    def by_role(work, *args):
+        for role in EDGES:
+            pl.when(me % 4 == role)(functools.partial(work, role, *args))
+
+    by_role(begin)
+    keeps = [
+        pltpu.make_async_copy(
+            own_ref.at[plane], full[plane].at[pl.ds(OWN * strip, strip)], keep_sem.at[plane]
+        )
+        for plane in range(planes)
+    ]
+    for keep in keeps:
+        keep.start()
+    share = phase_ref.shape[0] // len(chunks)
+    late = max(len(relays) for relays in RELAYS.values()) - 1
+    for step in range(len(chunks) + late):
+        if step < len(chunks):
+            table_rows(step * share, share, phase_ref, tables)
+        by_role(relay, step)
+    for plane in range(planes):
+        by_role(rest, plane)
+        keeps[plane].wait()
+    by_role(drain)
 
 
 def scatter_kernel(grad_ref, out_ref, total, held, send_sem, recv_sem, load_sem):
@@ -200,7 +271,7 @@
         def absorb(key, chunk):
             plane, lanes = chunks[chunk]
             for number, (source, half, target, _) in enumerate(edges):
-                if not ((source == OWN) if key is None else (source != OWN and source_key(role, source, half) == key)):
+                if not feeds(role, (source, half), key):
                     continue
                 count = strip if half == 0 else strip // 2
                 spot = held.at[number, plane, pl.ds(0, count), lanes]
@@ -279,21 +350,30 @@
     out_ref[0, pl.ds(pl.multiple_of(base + edge, 8), 8), :] = pltpu.roll(rows, 8 + past, 0)[:8]
 
 
-def gather(own, height):
+def gather(own, phase, height):
     planes, strip, columns = own.shape
+    edge = phase.shape[0]
+    left = jax.ShapeDtypeStruct((edge, 2 * edge), jnp.bfloat16)
+    right = jax.ShapeDtypeStruct((2 * edge, edge), jnp.bfloat16)
+    flat = jax.ShapeDtypeStruct((edge, edge), jnp.float32)
+    vmem = pl.BlockSpec(memory_space=pltpu.VMEM)
+    parts = planes * COLUMN_PARTS
     return pl.pallas_call(
         gather_kernel,
         name="gather",
-        out_shape=jax.ShapeDtypeStruct((planes, height, columns), jnp.float32),
-        in_specs=[pl.BlockSpec(memory_space=pltpu.VMEM)],
-        out_specs=pl.BlockSpec(memory_space=pl.ANY),
+        out_shape=[
+            jax.ShapeDtypeStruct((planes, height, columns), jnp.float32),
+            left, left, right, right, left, left, right, right, flat, flat,
+        ],
+        in_specs=[vmem, vmem],
+        out_specs=[pl.BlockSpec(memory_space=pl.ANY)] + [vmem] * 10,
         scratch_shapes=[
-            pltpu.SemaphoreType.DMA((MAX_EDGES, planes * COLUMN_PARTS)),
-            pltpu.SemaphoreType.DMA((12, planes * COLUMN_PARTS)),
-            pltpu.SemaphoreType.DMA,
+            pltpu.SemaphoreType.DMA((MAX_EDGES, parts)),
+            pltpu.SemaphoreType.DMA((12, parts)),
+            pltpu.SemaphoreType.DMA((planes,)),
         ],
         compiler_params=pltpu.CompilerParams(collective_id=0, has_side_effects=True),
-    )(own)
+    )(own, phase)
 
 
 def scatter(grads, strip):
@@ -331,23 +411,6 @@
     )(spot, source)
 
 
-def dft_mats(length, flip):
-    index = jnp.arange(length, dtype=jnp.int32)
-    angles = (index[:, None] * index[None, :] % length).astype(jnp.float32) * (
-        -2.0 * math.pi / length
-    )
-    factor = 1.0 / math.sqrt(length)
-    cos_table = (jnp.cos(angles) * factor).astype(jnp.bfloat16)
-    sin_table = (jnp.sin(angles) * factor).astype(jnp.bfloat16)
-    if flip:
-        sin_table = -sin_table
-    left_real = jnp.concatenate([cos_table, -sin_table], axis=1)
-    left_imag = jnp.concatenate([sin_table, cos_table], axis=1)
-    right_real = jnp.concatenate([cos_table, -sin_table], axis=0)
-    right_imag = jnp.concatenate([sin_table, cos_table], axis=0)
-    return (left_real, left_imag, right_real, right_imag)
-
-
 def transform(real_part, imag_part, mats):
     left_real, left_imag, right_real, right_imag = mats
     stacked = jnp.concatenate(
@@ -370,9 +433,8 @@
     return (a_real * b_real + a_imag * b_imag, a_real * b_imag - a_imag * b_real)
 
 
-def window_gradient(window, probe, amplitude, phase, forward, inverse):
-    prop_real = jnp.cos(phase)
-    prop_imag = jnp.sin(phase)
+def window_gradient(window, probe, amplitude, propagator, forward, inverse):
+    prop_real, prop_imag = propagator
     probe_real, probe_imag = (probe[0], probe[1])
     first_real, first_imag = (window[0], window[1])
     second_real, second_imag = (window[2], window[3])
@@ -401,13 +463,12 @@
     edge = probe.shape[1]
     half = strip // 2
     height = 5 * strip + half
-    forward = dft_mats(edge, False)
-    inverse = dft_mats(edge, True)
     own = object_field.reshape(4, strip, columns)
     spot = jnp.concatenate([row_offset + half, col_offset])
-    around = gather(own, height)
+    around, *tables = gather(own, phase, height)
+    forward, inverse, propagator = tables[:4], tables[4:8], tables[8:]
     window = local_move(extract_kernel, "extract", spot, around, (edge, edge))
-    grads = window_gradient(window, probe, amplitudes[0], phase, forward, inverse)
+    grads = window_gradient(window, probe, amplitudes[0], propagator, forward, inverse)
     spread = local_move(
         insert_kernel, "insert", spot, grads, (height, columns),
         [pltpu.VMEM((edge + 72, columns), jnp.float32)],

time: 167 us -> 166 us (level)
  other arithmetic: 16.2 us -> 7.92 us
  Pallas kernels: 123 us -> 131 us
    convert_element_type x1 -> x0, other arithmetic: 4.39 us -> none  [dft_mats(): sin_table = (jnp.sin(angles) * factor).astype(jnp.bfloat16)]
    pallas_call x1, Pallas kernels: 49.2 us -> 53.5 us  [gather(): pl.pallas_call(gather_kernel, name='gather', out_shape=[jax.ShapeDtypeStr...]
    neg x1 -> x0, other arithmetic: 4 us -> none  [dft_mats(): sin_table = -sin_table]
    sin x1 -> x0, local copies, waits for them, and re-layouts: 3.85 us -> none  [window_gradient(): prop_imag = jnp.sin(phase)]
    pallas_call x1, Pallas kernels: 54.7 us -> 58.1 us  [scatter(): pl.pallas_call(scatter_kernel, name='scatter', out_shape=jax.ShapeDtypeSt...]
    unnamed x10 -> x28, local copies, waits for them, and re-layouts: 2.41 us -> 5.27 us
where the time goes in v3:
time: 166 us; the launch traced here: 165 us
  Pallas kernels  131 us (79%)
  matrix products  19.6 us (12%)
  other arithmetic  7.92 us (5%)
  local copies, waits for them, and re-layouts  5.27 us (3%)
    pallas_call x1, Pallas kernels, scatter(): pl.pallas_call(scatter_kernel, name='scatter', out_shape=jax.ShapeDtypeSt...  58.1 us
    pallas_call x1, Pallas kernels, gather(): pl.pallas_call(gather_kernel, name='gather', out_shape=[jax.ShapeDtypeStr...  53.5 us
    pallas_call x2, Pallas kernels, local_move(): pl.pallas_call(kernel, name=name, out_shape=jax.ShapeDtypeStruct((planes,...  19.6 us
    dot_general x6, matrix products, transform(): jnp.dot(joined, right_real, preferred_element_type=jnp.float32)  5.39 us
    unnamed x28, local copies, waits for them, and re-layouts  5.27 us
    dot_general x6, matrix products, transform(): jnp.dot(joined, right_imag, preferred_element_type=jnp.float32)  4.89 us
    dot_general x6, matrix products, transform(): jnp.dot(left_real, stacked, preferred_element_type=jnp.float32)  4.77 us
    dot_general x6, matrix products, transform(): jnp.dot(left_imag, stacked, preferred_element_type=jnp.float32)  4.52 us

profile of v3, /device:TPU:1, one launch (start us, length us, event | category | flops | bytes accessed | tf_op | source)
XLA Modules:
  0.0 165.5 jit_solution(10161348797496861392)
XLA Ops:
  1.9 53.5 %gather.1 = (f32[4,704,768]{2,1,0:T(8,128)}, bf16[512,1024]{1,0:T(8,128)(2,1)}, bf16[512,1024]{1,0:T(8,128)(2,1)}, bf16[1024,512]{1,0:T(8,128)(2,1)}, bf16[1024,...) custom-call(f32[4,128,768]{2,1,0:T(8,128)} %bitcast.109, ...), custom_call_target="tpu_custom_call" | custom-call | tf_op jit(solution)/shard_map/gather/pallas_call | solution.py:361
  55.4 9.1 %extract.1 = f32[4,512,512]{2,1,0:T(8,128)} custom-call(s32[2]{0:T(128)} %pad_add_fusion.spot_ref, f32[4,704,768]{2,1,0:T(8,128)} %get-tuple-element.19.full_ref), custom_call_target="tpu_custom_call" | custom-call | tf_op jit(solution)/shard_map/extract/pallas_call | solution.py:400
  64.5 2.2 %fusion.2 = (bf16[512,512]{1,0:T(8,128)(2,1)S(1)}, bf16[512,512]{1,0:T(8,128)(2,1)S(1)}) fusion(f32[4,512,512]{2,1,0:T(8,128)} %extract.1, f32[2,512,512]{2,1,0:T(8,128)S(1)} %copy-done.5), kind=kLoop, calls=%fused_computation.37 | loop fusion | flops 2097152 | bytes 5242880 | tf_op jit(solution)/shard_map/convert_element_type | solution.py:417
  66.7 0.8 convolution_convert_fusion.10
  71.0 0.9 subtract_convert_fusion.3
  73.2 0.8 convolution_convert_fusion.9
  75.2 1.5 copy-done
  77.0 0.9 subtract_convert_fusion.2
  77.8 0.8 convolution_convert_fusion.6
  78.6 0.8 convolution_convert_fusion.7
  80.6 1.2 multiply_convert_fusion.1
  81.8 0.8 convolution_convert_fusion.4
  82.5 0.8 convolution_convert_fusion.5
  84.0 1.1 add_convert_fusion.1
  85.1 0.8 convolution_convert_fusion.2
  85.9 1.0 convolution_convert_fusion.3
  87.6 0.9 add_convert_fusion
  88.6 0.8 convolution_convert_fusion
  89.3 0.8 convolution_convert_fusion.1
  90.8 0.9 fusion.6
  91.7 2.4 %pad_maximum_fusion.grad_ref = f32[4,512,512]{2,1,0:T(8,128)} fusion(f32[1,512,512]{2,1,0:T(8,128)S(1)} %get-tuple-element.43, f32[1,512,512]{2,1,0:T(8,128)S(1)} %get-tuple-element.44, f32[1,512,512]{2,1,0:T(8,128)S(1)} %get-tuple-element.34, f32[1,512,512]{2,1,0:T(8,128)S(1)} %get-tuple-element.33), kind=kLoop, calls=%fused_computation | loop fusion | flops 3145728 | bytes 8388608 | tf_op jit(solution)/shard_map/stack | solution.py:458
  94.2 10.5 %insert.1.grad_ref = f32[4,704,768]{2,1,0:T(8,128)} custom-call(s32[2]{0:T(128)} %pad_add_fusion.spot_ref, f32[4,512,512]{2,1,0:T(8,128)} %pad_maximum_fusion.grad_ref), custom_call_target="tpu_custom_call" | custom-call | tf_op jit(solution)/shard_map/insert/pallas_call | solution.py:400
  104.7 58.1 %scatter.1 = f32[4,128,768]{2,1,0:T(8,128)} custom-call(f32[4,704,768]{2,1,0:T(8,128)} %insert.1.grad_ref), custom_call_target="tpu_custom_call" | custom-call | tf_op jit(solution)/shard_map/scatter/pallas_call | solution.py:381
  162.8 2.7 %multiply_subtract_fusion = f32[4,128,768]{2,1,0:T(8,128)} fusion(f32[4,128,768]{2,1,0:T(8,128)} %scatter.1, f32[2,2,128,768]{3,2,1,0:T(8,128)S(1)} %copy-done.1), kind=kLoop, calls=%fused_computation.1 | loop fusion | flops 786432 | bytes 4718592 | tf_op jit(solution)/shard_map/sub | solution.py:477
  (36 shorter events, 10.3 us)
Async XLA Ops:
  55.4 9.1 %copy-start.5 = (f32[2,512,512]{2,1,0:T(8,128)S(1)}, f32[2,512,512]{2,1,0:T(8,128)}, u32[]{:S(2)}) copy-start(f32[2,512,512]{2,1,0:T(8,128)} %param.10) | copy-start | bytes 6291460
  64.5 2.2 %copy-start.13 = (bf16[512,1024]{1,0:T(8,128)(2,1)S(1)}, bf16[512,1024]{1,0:T(8,128)(2,1)}, u32[]{:S(2)}) copy-start(bf16[512,1024]{1,0:T(8,128)(2,1)} %get-tuple-element.20) | copy-start | bytes 3145732
  66.7 1.2 copy-start.12
  67.9 1.2 copy-start.11
  69.2 1.2 copy-start.2
  69.2 1.5 copy-start.3
  69.2 1.9 %copy-start.4 = (f32[512,512]{1,0:T(8,128)S(1)}, f32[512,512]{1,0:T(8,128)}, u32[]{:S(2)}) copy-start(f32[512,512]{1,0:T(8,128)} %get-tuple-element.23) | copy-start | bytes 3145732
  71.0 1.2 copy-start.10
  71.9 1.3 copy-start.9
  73.2 1.2 copy-start.6
  74.5 2.2 %copy-start = (f32[4,512,512]{2,1,0:T(8,128)S(1)}, f32[4,512,512]{2,1,0:T(8,128)}, u32[]{:S(2)}) copy-start(f32[4,512,512]{2,1,0:T(8,128)} %extract.1) | copy-start | bytes 12582916
  74.5 2.5 %copy-start.8 = (bf16[1024,512]{1,0:T(8,128)(2,1)S(1)}, bf16[1024,512]{1,0:T(8,128)(2,1)}, u32[]{:S(2)}) copy-start(bf16[1024,512]{1,0:T(8,128)(2,1)} %get-tuple-element.26) | copy-start | bytes 3145732
  79.3 1.2 copy-start.7
  104.7 58.1 %copy-start.1 = (f32[2,2,128,768]{3,2,1,0:T(8,128)S(1)}, f32[2,2,128,768]{3,2,1,0:T(8,128)}, u32[]{:S(2)}) copy-start(f32[2,2,128,768]{3,2,1,0:T(8,128)} %param.6) | copy-start | bytes 4718596

commit v4 on v3

--- a/solution.py
+++ b/solution.py
@@ -105,9 +105,7 @@
 
 
 def table_rows(first, count, phase_ref, tables):
-    fore_left_real, fore_left_imag, fore_right_real, fore_right_imag = tables[0:4]
-    back_left_real, back_left_imag, back_right_real, back_right_imag = tables[4:8]
-    prop_real, prop_imag = tables[8:10]
+    left_real, left_imag, right_real, right_imag, prop_real, prop_imag = tables
     edge = phase_ref.shape[0]
     step = 16
 
@@ -124,22 +122,14 @@
         cosine = (jnp.cos(angles) * factor).astype(jnp.bfloat16)
         plain = jnp.sin(angles) * factor
         sine, minus = plain.astype(jnp.bfloat16), (-plain).astype(jnp.bfloat16)
-        fore_left_real[rows, low] = cosine
-        fore_left_real[rows, high] = minus
-        fore_left_imag[rows, low] = sine
-        fore_left_imag[rows, high] = cosine
-        fore_right_real[rows, :] = cosine
-        fore_right_real[more, :] = minus
-        fore_right_imag[rows, :] = sine
-        fore_right_imag[more, :] = cosine
-        back_left_real[rows, low] = cosine
-        back_left_real[rows, high] = sine
-        back_left_imag[rows, low] = minus
-        back_left_imag[rows, high] = cosine
-        back_right_real[rows, :] = cosine
-        back_right_real[more, :] = sine
-        back_right_imag[rows, :] = minus
-        back_right_imag[more, :] = cosine
+        left_real[rows, low] = cosine
+        left_real[rows, high] = minus
+        left_imag[rows, low] = sine
+        left_imag[rows, high] = cosine
+        right_real[rows, :] = cosine
+        right_real[more, :] = minus
+        right_imag[rows, :] = sine
+        right_imag[more, :] = cosine
         prop_real[rows, :] = jnp.cos(phase_ref[rows, :])
         prop_imag[rows, :] = jnp.sin(phase_ref[rows, :])
 
@@ -152,8 +142,8 @@
 
 
 def gather_kernel(own_ref, phase_ref, out_ref, *refs):
-    tables = refs[:10]
-    send_sem, recv_sem, keep_sem = refs[10:]
+    tables = refs[:6]
+    send_sem, recv_sem, keep_sem = refs[6:]
     full = [out_ref.at[plane] for plane in range(own_ref.shape[0])]
     planes, strip, columns = own_ref.shape
     chunks = chunks_of(planes, columns)
@@ -322,32 +312,29 @@
     @pl.loop(0, edge // step)
     def _(i):
         rows = full_ref[0, pl.ds(pl.multiple_of(base + i * step, 8), step + 8), :]
-        rows = pltpu.roll(rows, (step + 8 - past) % (step + 8), 0)[:step]
-        out_ref[0, pl.ds(i * step, step), :] = pltpu.roll(rows, turn, 1)[:, :edge]
-
-
-def insert_kernel(spot_ref, grad_ref, out_ref, wide_ref):
-    edge, columns = grad_ref.shape[-1], out_ref.shape[-1]
-    step = 64
+        rows = pltpu.roll(rows, turn, 1)[:, :edge]
+        out_ref[0, pl.ds(i * step, step), :] = pltpu.roll(rows, (step + 8 - past) % (step + 8), 0)[:step]
+
+
+def insert_kernel(spot_ref, grad_ref, out_ref, tall_ref):
+    edge, (height, columns) = grad_ref.shape[-1], out_ref.shape[1:]
+    step, lead = 64, height - edge
     past = spot_ref[0] % 8
     base = pl.multiple_of(spot_ref[0] - past, 8)
-    out_ref[...] = jnp.zeros_like(out_ref)
-    wide_ref[pl.ds(0, 8), :] = jnp.zeros((8, columns), jnp.float32)
-    wide_ref[pl.ds(edge + 8, step), :] = jnp.zeros((step, columns), jnp.float32)
-
-    @pl.loop(0, edge // step)
-    def _(i):
-        rows = grad_ref[0, pl.ds(i * step, step), :]
-        wide = jnp.concatenate([rows, jnp.zeros((step, columns - edge), jnp.float32)], axis=1)
-        wide_ref[pl.ds(i * step + 8, step), :] = pltpu.roll(wide, spot_ref[1], 1)
-
-    @pl.loop(0, edge // step)
-    def _(i):
-        rows = wide_ref[pl.ds(i * step, step + 8), :]
-        out_ref[0, pl.ds(pl.multiple_of(base + i * step, 8), step), :] = pltpu.roll(rows, step + past, 0)[:step]
-
-    rows = wide_ref[pl.ds(edge, 16), :]
-    out_ref[0, pl.ds(pl.multiple_of(base + edge, 8), 8), :] = pltpu.roll(rows, 8 + past, 0)[:8]
+    out_ref[0, pl.ds(0, lead), :] = jnp.zeros((lead, columns), jnp.float32)
+    out_ref[0, pl.ds(edge, lead), :] = jnp.zeros((lead, columns), jnp.float32)
+    tall_ref[pl.ds(0, 8), :] = jnp.zeros((8, edge), jnp.float32)
+    tall_ref[pl.ds(8, edge), :] = grad_ref[0]
+    tall_ref[pl.ds(edge + 8, 8), :] = jnp.zeros((8, edge), jnp.float32)
+
+    def move(i, count):
+        rows = tall_ref[pl.ds(i * step, count + 8), :]
+        rows = pltpu.roll(rows, count + past, 0)[:count]
+        wide = jnp.concatenate([rows, jnp.zeros((count, columns - edge), jnp.float32)], axis=1)
+        out_ref[0, pl.ds(pl.multiple_of(base + i * step, 8), count), :] = pltpu.roll(wide, spot_ref[1], 1)
+
+    pl.loop(0, edge // step)(lambda i: move(i, step))
+    move(edge // step, 8)
 
 
 def gather(own, phase, height):
@@ -363,10 +350,10 @@
         name="gather",
         out_shape=[
             jax.ShapeDtypeStruct((planes, height, columns), jnp.float32),
-            left, left, right, right, left, left, right, right, flat, flat,
+            left, left, right, right, flat, flat,
         ],
         in_specs=[vmem, vmem],
-        out_specs=[pl.BlockSpec(memory_space=pl.ANY)] + [vmem] * 10,
+        out_specs=[pl.BlockSpec(memory_space=pl.ANY)] + [vmem] * 6,
         scratch_shapes=[
             pltpu.SemaphoreType.DMA((MAX_EDGES, parts)),
             pltpu.SemaphoreType.DMA((12, parts)),
@@ -433,7 +420,7 @@
     return (a_real * b_real + a_imag * b_imag, a_real * b_imag - a_imag * b_real)
 
 
-def window_gradient(window, probe, amplitude, propagator, forward, inverse):
+def window_gradient(window, probe, amplitude, propagator, forward):
     prop_real, prop_imag = propagator
     probe_real, probe_imag = (probe[0], probe[1])
     first_real, first_imag = (window[0], window[1])
@@ -441,19 +428,19 @@
     exit_real, exit_imag = cmul(probe_real, probe_imag, first_real, first_imag)
     freq_real, freq_imag = transform(exit_real, exit_imag, forward)
     moved_real, moved_imag = cmul(freq_real, freq_imag, prop_real, prop_imag)
-    inner_real, inner_imag = transform(moved_real, moved_imag, inverse)
+    inner_imag, inner_real = transform(moved_imag, moved_real, forward)
     wave_real, wave_imag = cmul(inner_real, inner_imag, second_real, second_imag)
     far_real, far_imag = transform(wave_real, wave_imag, forward)
     modulus = jnp.sqrt(far_real * far_real + far_imag * far_imag)
     ratio = amplitude / jnp.maximum(modulus, 0.1)
     resid_real = far_real * (1.0 - ratio)
     resid_imag = far_imag * (1.0 - ratio)
-    back_real, back_imag = transform(resid_real, resid_imag, inverse)
+    back_imag, back_real = transform(resid_imag, resid_real, forward)
     grad2_real, grad2_imag = cmul_conj(inner_real, inner_imag, back_real, back_imag)
     mid_real, mid_imag = cmul_conj(second_real, second_imag, back_real, back_imag)
     spec_real, spec_imag = transform(mid_real, mid_imag, forward)
     unprop_real, unprop_imag = cmul_conj(prop_real, prop_imag, spec_real, spec_imag)
-    entry_real, entry_imag = transform(unprop_real, unprop_imag, inverse)
+    entry_imag, entry_real = transform(unprop_imag, unprop_real, forward)
     grad1_real, grad1_imag = cmul_conj(probe_real, probe_imag, entry_real, entry_imag)
     return jnp.stack([grad1_real, grad1_imag, grad2_real, grad2_imag])
 
@@ -466,12 +453,12 @@
     own = object_field.reshape(4, strip, columns)
     spot = jnp.concatenate([row_offset + half, col_offset])
     around, *tables = gather(own, phase, height)
-    forward, inverse, propagator = tables[:4], tables[4:8], tables[8:]
+    forward, propagator = tables[:4], tables[4:]
     window = local_move(extract_kernel, "extract", spot, around, (edge, edge))
-    grads = window_gradient(window, probe, amplitudes[0], propagator, forward, inverse)
+    grads = window_gradient(window, probe, amplitudes[0], propagator, forward)
     spread = local_move(
         insert_kernel, "insert", spot, grads, (height, columns),
-        [pltpu.VMEM((edge + 72, columns), jnp.float32)],
+        [pltpu.VMEM((edge + 16, edge), jnp.float32)],
     )
     total = scatter(spread, strip)
     return (own - 0.5 * total).reshape(object_field.shape)

time: 166 us -> 163 us (0.982)
  Pallas kernels: 131 us -> 129 us
    unnamed x28 -> x20, local copies, waits for them, and re-layouts: 5.27 us -> 3.98 us
where the time goes in v4:
time: 163 us; the launch traced here: 162 us
  Pallas kernels  129 us (79%)
  matrix products  19.5 us (12%)
  other arithmetic  7.92 us (5%)
  local copies, waits for them, and re-layouts  3.98 us (2%)
    pallas_call x1, Pallas kernels, scatter(): pl.pallas_call(scatter_kernel, name='scatter', out_shape=jax.ShapeDtypeSt...  58 us
    pallas_call x1, Pallas kernels, gather(): pl.pallas_call(gather_kernel, name='gather', out_shape=[jax.ShapeDtypeStr...  52.3 us
    pallas_call x2, Pallas kernels, local_move(): pl.pallas_call(kernel, name=name, out_shape=jax.ShapeDtypeStruct((planes,...  19 us
    dot_general x6, matrix products, transform(): jnp.dot(joined, right_imag, preferred_element_type=jnp.float32)  5.53 us
    dot_general x6, matrix products, transform(): jnp.dot(left_real, stacked, preferred_element_type=jnp.float32)  4.77 us
    dot_general x6, matrix products, transform(): jnp.dot(joined, right_real, preferred_element_type=jnp.float32)  4.66 us
    dot_general x6, matrix products, transform(): jnp.dot(left_imag, stacked, preferred_element_type=jnp.float32)  4.52 us
    unnamed x20, local copies, waits for them, and re-layouts  3.98 us

profile of v4, /device:TPU:1, one launch (start us, length us, event | category | flops | bytes accessed | tf_op | source)
XLA Modules:
  0.0 162.2 jit_solution(12595054341907436566)
XLA Ops:
  1.9 52.3 %gather.1 = (f32[4,704,768]{2,1,0:T(8,128)}, bf16[512,1024]{1,0:T(8,128)(2,1)}, bf16[512,1024]{1,0:T(8,128)(2,1)}, bf16[1024,512]{1,0:T(8,128)(2,1)}, bf16[1024,...) custom-call(f32[4,128,768]{2,1,0:T(8,128)} %bitcast.109, f32[512,512]{1,0:T(8,128)} %phase_ref.1), custom_call_target="tpu_custom_call" | custom-call | tf_op jit(solution)/shard_map/gather/pallas_call | solution.py:348
  54.2 9.6 %extract.1 = f32[4,512,512]{2,1,0:T(8,128)} custom-call(s32[2]{0:T(128)} %pad_add_fusion.spot_ref, f32[4,704,768]{2,1,0:T(8,128)} %get-tuple-element.14.full_ref), custom_call_target="tpu_custom_call" | custom-call | tf_op jit(solution)/shard_map/extract/pallas_call | solution.py:387
  63.8 2.2 %fusion.2 = (bf16[512,512]{1,0:T(8,128)(2,1)S(1)}, bf16[512,512]{1,0:T(8,128)(2,1)S(1)}) fusion(f32[4,512,512]{2,1,0:T(8,128)} %extract.1, f32[2,512,512]{2,1,0:T(8,128)S(1)} %copy-done.5), kind=kLoop, calls=%fused_computation.37 | loop fusion | flops 2097152 | bytes 5242880 | tf_op jit(solution)/shard_map/convert_element_type | solution.py:404
  66.0 0.8 convolution_convert_fusion.10
  67.2 0.8 convolution_convert_fusion.11
  70.3 0.9 add_convert_fusion.3
  71.2 0.8 convolution_convert_fusion.8
  71.9 0.8 convolution_convert_fusion.9
  73.5 1.4 copy-done
  74.9 0.9 subtract_convert_fusion.2
  76.5 0.8 convolution_convert_fusion.7
  78.5 1.2 multiply_convert_fusion.1
  80.5 0.8 convolution_convert_fusion.5
  82.0 1.1 add_convert_fusion.1
  83.1 0.8 convolution_convert_fusion.2
  83.8 1.0 convolution_convert_fusion.3
  85.6 0.9 subtract_convert_fusion
  86.5 0.8 convolution_convert_fusion
  87.2 0.8 convolution_convert_fusion.1
  88.7 0.9 fusion.6
  89.6 2.4 %pad_maximum_fusion.grad_ref = f32[4,512,512]{2,1,0:T(8,128)} fusion(f32[1,512,512]{2,1,0:T(8,128)S(1)} %get-tuple-element.35, f32[1,512,512]{2,1,0:T(8,128)S(1)} %get-tuple-element.36, f32[1,512,512]{2,1,0:T(8,128)S(1)} %get-tuple-element.26, f32[1,512,512]{2,1,0:T(8,128)S(1)} %get-tuple-element.25), kind=kLoop, calls=%fused_computation | loop fusion | flops 3145728 | bytes 8388608 | tf_op jit(solution)/shard_map/stack | solution.py:445
  92.1 9.4 %insert.1.grad_ref = f32[4,704,768]{2,1,0:T(8,128)} custom-call(s32[2]{0:T(128)} %pad_add_fusion.spot_ref, f32[4,512,512]{2,1,0:T(8,128)} %pad_maximum_fusion.grad_ref), custom_call_target="tpu_custom_call" | custom-call | tf_op jit(solution)/shard_map/insert/pallas_call | solution.py:387
  101.5 58.0 %scatter.1 = f32[4,128,768]{2,1,0:T(8,128)} custom-call(f32[4,704,768]{2,1,0:T(8,128)} %insert.1.grad_ref), custom_call_target="tpu_custom_call" | custom-call | tf_op jit(solution)/shard_map/scatter/pallas_call | solution.py:368
  159.5 2.7 %multiply_subtract_fusion = f32[4,128,768]{2,1,0:T(8,128)} fusion(f32[4,128,768]{2,1,0:T(8,128)} %scatter.1, f32[2,2,128,768]{3,2,1,0:T(8,128)S(1)} %copy-done.1), kind=kLoop, calls=%fused_computation.1 | loop fusion | flops 786432 | bytes 4718592 | tf_op jit(solution)/shard_map/sub | solution.py:464
  (28 shorter events, 9.0 us)
Async XLA Ops:
  54.2 9.6 %copy-start.5 = (f32[2,512,512]{2,1,0:T(8,128)S(1)}, f32[2,512,512]{2,1,0:T(8,128)}, u32[]{:S(2)}) copy-start(f32[2,512,512]{2,1,0:T(8,128)} %param.10) | copy-start | bytes 6291460
  63.8 2.2 %copy-start.9 = (bf16[512,1024]{1,0:T(8,128)(2,1)S(1)}, bf16[512,1024]{1,0:T(8,128)(2,1)}, u32[]{:S(2)}) copy-start(bf16[512,1024]{1,0:T(8,128)(2,1)} %get-tuple-element.15) | copy-start | bytes 3145732
  66.0 1.2 copy-start.8
  67.2 1.2 copy-start.6
  68.4 1.2 copy-start.2
  68.4 1.5 copy-start.3
  68.5 1.9 %copy-start.4 = (f32[512,512]{1,0:T(8,128)S(1)}, f32[512,512]{1,0:T(8,128)}, u32[]{:S(2)}) copy-start(f32[512,512]{1,0:T(8,128)} %get-tuple-element.17) | copy-start | bytes 3145732
  72.7 2.2 %copy-start = (f32[4,512,512]{2,1,0:T(8,128)S(1)}, f32[4,512,512]{2,1,0:T(8,128)}, u32[]{:S(2)}) copy-start(f32[4,512,512]{2,1,0:T(8,128)} %extract.1) | copy-start | bytes 12582916
  77.3 1.2 copy-start.7
  101.5 58.0 %copy-start.1 = (f32[2,2,128,768]{3,2,1,0:T(8,128)S(1)}, f32[2,2,128,768]{3,2,1,0:T(8,128)}, u32[]{:S(2)}) copy-start(f32[2,2,128,768]{3,2,1,0:T(8,128)} %param.6) | copy-start | bytes 4718596
